TPU v7x, 128 devices: a whole 4x4x4 slice. The times are simulated.
128 devices in a mesh: pipe: 16 (over y_lo, z, core), seq: 8 (over x, y_hi).
Axes of the slice: x: 4, y: 4 (y_hi: 2, y_lo: 2; y = y_hi * 2 + y_lo), z: 4, core: 2. Of those that a mesh axis runs over, the one named last changes fastest.
Arguments:
- x_fwd: float32 [16, 1024, 2048], P('pipe', 'seq'), may hold values from -12 to 12
- x_bwd: float32 [16, 1024, 2048], P('pipe', 'seq'), may hold values from -12 to 12
- grad_in: float32 [16, 1024, 2048], P('pipe', 'seq'), may hold values from -6 to 6
- gain: float32 [16, 2048], P('pipe'), may hold values from 0.25 to 1.75
- w_query: bfloat16 [16, 2048, 2048], P('pipe', None, 'seq'), may hold values from -2 to 2
- w_key: bfloat16 [16, 2048, 2048], P('pipe', None, 'seq'), may hold values from -2 to 2
- w_value: bfloat16 [16, 2048, 2048], P('pipe', None, 'seq'), may hold values from -0.125 to 0.125
- w_out: bfloat16 [16, 2048, 2048], P('pipe', None, 'seq'), may hold values from -0.125 to 0.125
Outputs:
- act_next: float32 [16, 1024, 2048], P('pipe', 'seq')
- grad_prev: float32 [16, 1024, 2048], P('pipe', 'seq')
All inputs are finite; a program needn't handle non-finite values.
Results may differ from a plain program's by a relative error of at most 0.012.
The roundings to bfloat16 on the way count: a program that leaves them out, or rounds other values in their place, can miss the bound.
Values may be sent and summed in bfloat16 or wider, within the bound.
A program may use at most 192 MiB of HBM per device.

v0:
```python
import jax
import jax.numpy as jnp
from jax import lax
from jax.sharding import PartitionSpec as P

HD = 128


def passed_along(value, axis, steps):
    count = lax.axis_size(axis)
    pairs = [(source, (source + steps) % count) for source in range(count)]
    return lax.ppermute(value, axis, pairs)


def rope_tables(positions):
    half_dim = HD // 2
    inverse = 10000.0 ** (-(jnp.arange(half_dim).astype(jnp.float32) * 2.0 / HD))
    angles = positions.astype(jnp.float32)[:, None] * inverse[None, :]
    return (jnp.cos(angles)[:, None, :], jnp.sin(angles)[:, None, :])


def rotate(values, cosine, sine_table):
    shaped = values.reshape(values.shape[0], -1, HD)
    first_half = shaped[..., : HD // 2]
    second_half = shaped[..., HD // 2 :]
    output = jnp.concatenate(
        [
            first_half * cosine - second_half * sine_table,
            second_half * cosine + first_half * sine_table,
        ],
        -1,
    )
    return output.reshape(values.shape)


def rotate_back(values, cosine, sine_table):
    shaped = values.reshape(values.shape[0], -1, HD)
    first_half = shaped[..., : HD // 2]
    second_half = shaped[..., HD // 2 :]
    output = jnp.concatenate(
        [
            first_half * cosine + second_half * sine_table,
            second_half * cosine - first_half * sine_table,
        ],
        -1,
    )
    return output.reshape(values.shape)


def normalize(inputs, gain_row):
    inv_rms = lax.rsqrt(jnp.mean(inputs * inputs, -1, keepdims=True) + 1e-05)
    return ((inputs * inv_rms * gain_row).astype(jnp.bfloat16), inv_rms)


def times_t(left, right):
    return lax.dot_general(
        left, right, (((1,), (1,)), ((), ())), preferred_element_type=jnp.float32
    )


def split_heads(values):
    return values.reshape(values.shape[0], -1, HD)


def attend(query, key_rows, value_rows):
    length = query.shape[0]
    score_scale = HD ** (-0.5)
    key_heads = split_heads(key_rows)
    value_heads = split_heads(value_rows)
    query_blocks = split_heads(query).reshape(length // length, length, -1, HD)

    def one_block(query_block):
        scores = (
            jnp.einsum("qhd,khd->hqk", query_block, key_heads, preferred_element_type=jnp.float32)
            * score_scale
        )
        probs = jax.nn.softmax(scores, axis=-1)
        output = jnp.einsum(
            "hqk,khd->qhd",
            probs.astype(jnp.bfloat16),
            value_heads,
            preferred_element_type=jnp.float32,
        )
        return output.astype(jnp.bfloat16)

    return lax.map(one_block, query_blocks).reshape(length, -1)


def attend_back(query, key_rows, value_rows, grad_out, cosine, sine_table):
    length = query.shape[0]
    score_scale = HD ** (-0.5)
    key_heads = split_heads(key_rows)
    value_heads = split_heads(value_rows)
    query_blocks = split_heads(query).reshape(length // length, length, -1, HD)
    grad_blocks = split_heads(grad_out).reshape(length // length, length, -1, HD)

    def step(totals, operands):
        query_block, grad_block = operands
        scores = (
            jnp.einsum("qhd,khd->hqk", query_block, key_heads, preferred_element_type=jnp.float32)
            * score_scale
        )
        probs = jax.nn.softmax(scores, axis=-1)
        value_grad = jnp.einsum(
            "hqk,qhd->khd",
            probs.astype(jnp.bfloat16),
            grad_block,
            preferred_element_type=jnp.float32,
        )
        prob_grad = jnp.einsum(
            "qhd,khd->hqk", grad_block, value_heads, preferred_element_type=jnp.float32
        )
        row_delta = jnp.sum(probs * prob_grad, -1, keepdims=True)
        score_grad = (probs * (prob_grad - row_delta) * score_scale).astype(jnp.bfloat16)
        query_grad = jnp.einsum(
            "hqk,khd->qhd", score_grad, key_heads, preferred_element_type=jnp.float32
        )
        key_grad = jnp.einsum(
            "hqk,qhd->khd", score_grad, query_block, preferred_element_type=jnp.float32
        )
        return ((totals[0] + key_grad, totals[1] + value_grad), query_grad)

    zero_heads = jnp.zeros(key_heads.shape, jnp.float32)
    (key_total, value_total), query_grads = lax.scan(
        step, (zero_heads, zero_heads), (query_blocks, grad_blocks)
    )
    query_grad = rotate_back(query_grads.reshape(length, -1), cosine, sine_table).astype(
        jnp.bfloat16
    )
    key_grad = rotate_back(key_total.reshape(length, -1), cosine, sine_table).astype(jnp.bfloat16)
    return (query_grad, key_grad, value_total.reshape(length, -1).astype(jnp.bfloat16))


def to_tokens(values):
    return lax.all_to_all(values, "seq", split_axis=1, concat_axis=2, tiled=True)


def shards(x_fwd, x_bwd, grad_in, gain, w_query, w_key, w_value, w_out):
    act_in = x_fwd[0]
    saved_in = x_bwd[0]
    grad = grad_in[0]
    gain_row = gain[0]
    local_rows = act_in.shape[0]
    length = local_rows * lax.axis_size("seq")
    normed_fwd, inv_fwd = normalize(act_in, gain_row)
    normed_bwd, inv_bwd = normalize(saved_in, gain_row)
    grad_low = grad.astype(jnp.bfloat16)
    full_cos, full_sin = rope_tables(jnp.arange(length))
    all_query, all_key, all_value, all_out = (
        lax.all_gather(w_query[0], "seq", axis=1, tiled=True),
        lax.all_gather(w_key[0], "seq", axis=1, tiled=True),
        lax.all_gather(w_value[0], "seq", axis=1, tiled=True),
        lax.all_gather(w_out[0], "seq", axis=1, tiled=True),
    )
    local_cos, local_sin = rope_tables(lax.axis_index("seq") * local_rows + jnp.arange(local_rows))

    def project_local(normed):
        query = rotate(
            jnp.dot(normed, all_query, preferred_element_type=jnp.float32), local_cos, local_sin
        ).astype(jnp.bfloat16)
        key_rows = rotate(
            jnp.dot(normed, all_key, preferred_element_type=jnp.float32), local_cos, local_sin
        ).astype(jnp.bfloat16)
        value_rows = jnp.dot(normed, all_value, preferred_element_type=jnp.float32).astype(
            jnp.bfloat16
        )
        return [query, key_rows, value_rows]

    attn_grad = jnp.dot(grad_low, all_out, preferred_element_type=jnp.float32).astype(jnp.bfloat16)
    pieces = jnp.stack(project_local(normed_fwd) + project_local(normed_bwd) + [attn_grad])
    head_view = lax.all_to_all(pieces, "seq", split_axis=2, concat_axis=1, tiled=True)
    attn = attend(head_view[0], head_view[1], head_view[2])
    attn_tokens = to_tokens(attn[None])[0]
    branch = times_t(attn_tokens, all_out)
    query_grad, key_grad, value_grad = attend_back(
        head_view[3], head_view[4], head_view[5], head_view[6], full_cos, full_sin
    )
    grad_tokens = to_tokens(jnp.stack([query_grad, key_grad, value_grad]))
    d_normed = (
        times_t(grad_tokens[0], all_query)
        + times_t(grad_tokens[1], all_key)
        + times_t(grad_tokens[2], all_value)
    )
    act_out = act_in + branch
    gain_grad = d_normed * gain_row
    d_input = inv_bwd * gain_grad - saved_in * inv_bwd * inv_bwd * inv_bwd * jnp.mean(
        saved_in * gain_grad, -1, keepdims=True
    )
    sent_forward = passed_along(act_out.astype(jnp.bfloat16), "pipe", 1).astype(act_out.dtype)
    sent_backward = passed_along((grad + d_input).astype(jnp.bfloat16), "pipe", -1).astype(
        jnp.float32
    )
    return (sent_forward[None], sent_backward[None])


def solution(mesh):
    placed = (
        P("pipe", "seq", None),
        P("pipe", "seq", None),
        P("pipe", "seq", None),
        P("pipe", None),
        P("pipe", None, "seq"),
        P("pipe", None, "seq"),
        P("pipe", None, "seq"),
        P("pipe", None, "seq"),
    )
    return jax.shard_map(
        shards,
        mesh=mesh,
        in_specs=placed,
        out_specs=(P("pipe", "seq", None), P("pipe", "seq", None)),
        check_vma=False,
    )
```

profile of v0, /device:TPU:0, one launch (start us, length us, event | category | flops | bytes accessed | tf_op | source)
XLA Modules:
  0.0 762.9 jit_solution(12762140533666074192)
XLA Ops:
  13.0 119.1 %all-gather.11.cloned.1.call-done = bf16[1,2048,2048]{2,1,0:T(8,128)(2,1)} async-done(((bf16[1,2048,256]{2,1,0:T(8,128)(2,1)}), bf16[1,2048,2048]{2,1,0:T(8,128)(2,1)}) %all-gather.11.cloned.1.call-update) | async-done | bytes 8388624 | tf_op jit(solution)/shard_map/all_gather | solution.py:151
  132.1 12.4 %copy.67 = bf16[2048,2048]{1,0:T(8,128)(2,1)} copy(bf16[2048,2048]{0,1:T(8,128)(2,1)} %bitcast.212) | data formatting | bytes 16777216 | tf_op jit(solution)/shard_map/dot_general | solution.py:162
  144.5 108.1 %all-gather.9.cloned.1.call-done = bf16[1,2048,2048]{2,1,0:T(8,128)(2,1)} async-done(((bf16[1,2048,256]{2,1,0:T(8,128)(2,1)}), bf16[1,2048,2048]{2,1,0:T(8,128)(2,1)}) %all-gather.9.cloned.1.call-update) | async-done | bytes 8388624 | tf_op jit(solution)/shard_map/all_gather | solution.py:150
  252.6 12.4 %copy.66 = bf16[2048,2048]{1,0:T(8,128)(2,1)} copy(bf16[2048,2048]{0,1:T(8,128)(2,1)} %bitcast.213) | data formatting | bytes 16777216 | tf_op jit(solution)/shard_map/dot_general | solution.py:159
  265.0 6.3 fusion.112
  271.3 2.5 fusion.116
  274.0 2.5 fusion.114
  276.4 2.5 fusion.118
  282.7 2.2 pad_maximum_fusion.1
  292.8 80.3 %all-gather.13.cloned.1.call-done = bf16[1,2048,2048]{2,1,0:T(8,128)(2,1)} async-done(((bf16[1,2048,256]{2,1,0:T(8,128)(2,1)}), bf16[1,2048,2048]{2,1,0:T(8,128)(2,1)}) %all-gather.13.cloned.1.call-update) | async-done | bytes 8388624 | tf_op jit(solution)/shard_map/all_gather | solution.py:152
  373.1 5.6 fusion.76
  380.5 2.6 fusion.70
  383.0 110.4 %all-gather.15.cloned.1.call-done = bf16[1,2048,2048]{2,1,0:T(8,128)(2,1)} async-done(((bf16[1,2048,256]{2,1,0:T(8,128)(2,1)}), bf16[1,2048,2048]{2,1,0:T(8,128)(2,1)}) %all-gather.15.cloned.1.call-update) | async-done | bytes 8388624 | tf_op jit(solution)/shard_map/all_gather | solution.py:153
  493.5 5.5 fusion.64
  498.9 6.5 copy.72
  505.4 4.5 all-to-all-start
  511.7 56.7 %all-to-all-done = bf16[7,128,2048]{1,0,2:T(8,128)(2,1)} async-done(((bf16[7,128,2048]{1,0,2:T(8,128)(2,1)}), bf16[7,128,2048]{1,0,2:T(8,128)(2,1)}, u32[]{:S(2)}, u32[]{:S(2)}) %all-to-all-start) | async-done | bytes 3670048 | tf_op jit(solution)/shard_map/all_to_all | solution.py:171
  568.4 4.8 copy.105
  575.1 2.1 reshape_squeeze.15
  577.2 2.1 squeeze.56
  581.3 2.1 reshape_squeeze.14
  583.4 5.7 fusion.127
  589.1 7.2 fusion.124
  596.3 5.9 fusion.86
  602.2 14.8 %fusion.82 = f32[1024,2,128]{0,2,1:T(8,128)} fusion(bf16[1024,2,128]{0,2,1:T(8,128)(2,1)} %squeeze.55, f32[2,1024,1024]{1,2,0:T(8,128)} %fusion.127, f32[2,1024,1024]{1,2,0:T(8,128)} %get-tuple-element.78, f32[2,1024]{1,0:T(2,128)S(1)} %get-tuple-element.77), kind=kOutput, calls=%fused_computation.52 | convolution fusion | flops 551554048 | bytes 18358272 | tf_op jit(solution)/shard_map/while/body/eval_jaxpr/hqk,qhd->khd/dot_general | solution.py:118
  617.0 14.8 %fusion.79 = f32[1024,2,128]{0,2,1:T(8,128)} fusion(bf16[1024,2,128]{0,2,1:T(8,128)(2,1)} %reshape_squeeze.14, f32[2,1024,1024]{1,2,0:T(8,128)} %fusion.127, f32[2,1024,1024]{1,2,0:T(8,128)} %get-tuple-element.78, f32[2,1024]{1,0:T(2,128)S(1)} %get-tuple-element.77), kind=kOutput, calls=%fused_computation.51 | convolution fusion | flops 551554048 | bytes 18358272 | tf_op jit(solution)/shard_map/while/body/eval_jaxpr/hqk,khd->qhd/dot_general | solution.py:115
  631.8 2.1 reshape_squeeze.13
  633.9 2.1 squeeze.53
  638.0 7.2 fusion.123
  645.2 5.1 fusion.85
  650.3 3.6 copy.77
  654.4 5.6 reduce
  662.0 4.4 all-to-all-start.1
  666.4 2.7 add_convert_fusion.1
  669.9 3.6 copy.88
  673.5 3.6 copy.86
  678.9 3.6 copy.87
  682.5 6.0 pad_maximum_fusion
  688.5 7.2 all-to-all-start.2
  695.6 3.5 reshape.322
  699.1 2.1 copy.103
  703.2 7.3 fusion.58
  710.8 13.4 %all-to-all-done.2 = bf16[3,1024,256]{2,0,1:T(4,128)(2,1)} async-done(((bf16[3,1024,256]{2,0,1:T(4,128)(2,1)}), bf16[3,1024,256]{2,0,1:T(4,128)(2,1)}, u32[]{:S(2)}, u32[]{:S(2)}) %all-to-all-start.2) | async-done | bytes 1572896 | tf_op jit(solution)/shard_map/all_to_all | solution.py:135
  731.0 6.6 fusion.13
  737.6 6.5 fusion.37
  744.1 3.0 fusion.91
  748.2 2.1 bitcast_convert_fusion.3
  750.3 4.6 collective-permute-done.1
  (73 shorter events, 43.5 us)
Async XLA Ops:
  7.2 124.9 %all-gather.11.cloned.1.call-start = ((), (), s32[]{:S(2)}) async-start(), calls=%async_computation.4 | async-start | bytes 9437184 | tf_op jit(solution)/shard_map/all_gather | solution.py:151
  7.9 244.7 %all-gather.9.cloned.1.call-start = ((), (), s32[]{:S(2)}) async-start(), calls=%async_computation.3 | async-start | bytes 9437184 | tf_op jit(solution)/shard_map/all_gather | solution.py:150
  8.6 364.5 %all-gather.13.cloned.1.call-start = ((), (), s32[]{:S(2)}) async-start(), calls=%async_computation.5 | async-start | bytes 9437184 | tf_op jit(solution)/shard_map/all_gather | solution.py:152
  9.4 484.1 %all-gather.15.cloned.1.call-start = ((), (), s32[]{:S(2)}) async-start(), calls=%async_computation.6 | async-start | bytes 9437184 | tf_op jit(solution)/shard_map/all_gather | solution.py:153
  252.6 12.4 %copy-start.2 = (f32[1,128,2048]{2,1,0:T(8,128)S(1)}, f32[1,128,2048]{2,1,0:T(8,128)}, u32[]{:S(2)}) copy-start(f32[1,128,2048]{2,1,0:T(8,128)} %param.9) | copy-start | bytes 3145732
  252.6 12.4 %copy-start.7 = (f32[1,2048]{1,0:T(1,128)S(1)}, f32[1,2048]{1,0:T(1,128)}, u32[]{:S(2)}) copy-start(f32[1,2048]{1,0:T(1,128)} %param.11) | copy-start | bytes 24580
  265.0 6.3 copy-start.1
  265.0 6.3 copy-start.3
  265.0 8.8 %slice-start.2 = ((s8[8388608]{0:T(1024)(128)(4,1)}), s8[4194304]{0:T(1024)(128)(4,1)S(1)}, s32[]{:S(2)}) async-start(s8[8388608]{0:T(1024)(128)(4,1)} %bitcast.208), calls=%async_computation.9 | async-start | bytes 8388608
  271.3 2.7 slice-start.3
  373.1 7.3 copy-start
  380.5 113.0 %copy-start.4 = (f32[1,128,2048]{2,1,0:T(8,128)S(1)}, f32[1,128,2048]{2,1,0:T(8,128)}, u32[]{:S(2)}) copy-start(f32[1,128,2048]{2,1,0:T(8,128)} %param.10) | copy-start | bytes 3145732
  505.4 63.0 %all-to-all-start = ((bf16[7,128,2048]{1,0,2:T(8,128)(2,1)}), bf16[7,128,2048]{1,0,2:T(8,128)(2,1)}, u32[]{:S(2)}, u32[]{:S(2)}) async-start(bf16[7,128,2048]{1,0,2:T(8,128)(2,1)} %copy.72), calls=%async_computation | async-start | bytes 8388608 | tf_op jit(solution)/shard_map/all_to_all | solution.py:171
  662.0 26.4 %all-to-all-start.1 = ((bf16[8,2,16384]{2,1,0:T(2,128)(2,1)}), bf16[8,2,16384]{2,1,0:T(2,128)(2,1)}, u32[]{:S(2)}, u32[]{:S(2)}) async-start(bf16[8,2,16384]{2,1,0:T(2,128)(2,1)} %reshape.321), calls=%async_computation.1 | async-start | bytes 1048576 | tf_op jit(solution)/shard_map/all_to_all | solution.py:135
  688.5 35.7 %all-to-all-start.2 = ((bf16[3,1024,256]{2,0,1:T(4,128)(2,1)}), bf16[3,1024,256]{2,0,1:T(4,128)(2,1)}, u32[]{:S(2)}, u32[]{:S(2)}) async-start(bf16[3,1024,256]{2,0,1:T(4,128)(2,1)} %pad_maximum_fusion), calls=%async_computation.2 | async-start | bytes 4194304 | tf_op jit(solution)/shard_map/all_to_all | solution.py:135
  710.5 37.6 %collective-permute-start = (bf16[128,2048]{1,0:T(8,128)(2,1)}, bf16[128,2048]{1,0:T(8,128)(2,1)}, u32[]{:S(2)}, u32[]{:S(2)}) collective-permute-start(bf16[128,2048]{1,0:T(8,128)(2,1)} %fusion.58), channel_id=1, source_target_pairs={{0,8},{8,16},{16,24},{24,32},{32,40},{40,48},{48,56},{56,64},{64,7... | collective-permute-start | bytes 1572872 | tf_op jit(solution)/shard_map/ppermute | solution.py:12
  730.9 6.6 copy-start.6
  730.9 13.1 %slice-start = ((s8[8388608]{0:T(1024)(128)(4,1)}), s8[4194304]{0:T(1024)(128)(4,1)S(1)}, s32[]{:S(2)}) async-start(s8[8388608]{0:T(1024)(128)(4,1)} %bitcast.204), calls=%async_computation.7 | async-start | bytes 8388608
  730.9 13.1 %copy-start.5 = (bf16[1,128,8,256]{1,3,2,0:T(8,128)(2,1)S(1)}, bf16[1,128,8,256]{1,3,2,0:T(8,128)(2,1)}, u32[]{:S(2)}) copy-start(bf16[1,128,8,256]{1,3,2,0:T(8,128)(2,1)} %copy.92) | copy-start | bytes 1572868
  737.6 6.5 slice-start.1
  747.4 7.4 collective-permute-start.1
Sparse Core Ops, SparseCore 0:
  10.2 121.9 all-gather.10
  134.3 118.2 all-gather.8
  254.8 118.3 all-gather.12
  375.2 118.2 all-gather.14
where the time goes:
time: 777 us; the launch traced here: 763 us
  waiting for transfers between devices  495 us (64%)
  matrix products  111 us (14%)
  local copies, waits for them, and re-layouts  95 us (12%)
  other arithmetic  29.8 us (4%)
  starting transfers between devices  17.2 us (2%)
  between operations  14.5 us (2%)
    all_gather x1, waiting for transfers between devices, shards(): lax.all_gather(w_key[0], 'seq', axis=1, tiled=True)  119 us
    all_gather x1, waiting for transfers between devices, shards(): lax.all_gather(w_out[0], 'seq', axis=1, tiled=True)  110 us
    all_gather x1, waiting for transfers between devices, shards(): lax.all_gather(w_query[0], 'seq', axis=1, tiled=True)  108 us
    all_gather x1, waiting for transfers between devices, shards(): lax.all_gather(w_value[0], 'seq', axis=1, tiled=True)  80.3 us
    all_to_all x1, waiting for transfers between devices, shards(): lax.all_to_all(pieces, 'seq', split_axis=2, concat_axis=1, tiled=True)  56.7 us
    dot_general x4, matrix products, times_t(): lax.dot_general(left, right, (((1,), (1,)), ((), ())), preferred_element_...  23.3 us
  transfers between devices with their start and end apart: 9, of which 7 were waited for; matrix products, arithmetic and copies ran while one was open for 17% of the time, Pallas kernels for 0%

commit v1 on v0

--- a/solution.py
+++ b/solution.py
@@ -129,10 +129,6 @@
     )
     key_grad = rotate_back(key_total.reshape(length, -1), cosine, sine_table).astype(jnp.bfloat16)
     return (query_grad, key_grad, value_total.reshape(length, -1).astype(jnp.bfloat16))
-
-
-def to_tokens(values):
-    return lax.all_to_all(values, "seq", split_axis=1, concat_axis=2, tiled=True)
 
 
 def shards(x_fwd, x_bwd, grad_in, gain, w_query, w_key, w_value, w_out):
@@ -146,42 +142,42 @@
     normed_bwd, inv_bwd = normalize(saved_in, gain_row)
     grad_low = grad.astype(jnp.bfloat16)
     full_cos, full_sin = rope_tables(jnp.arange(length))
-    all_query, all_key, all_value, all_out = (
-        lax.all_gather(w_query[0], "seq", axis=1, tiled=True),
-        lax.all_gather(w_key[0], "seq", axis=1, tiled=True),
-        lax.all_gather(w_value[0], "seq", axis=1, tiled=True),
-        lax.all_gather(w_out[0], "seq", axis=1, tiled=True),
-    )
-    local_cos, local_sin = rope_tables(lax.axis_index("seq") * local_rows + jnp.arange(local_rows))
-
-    def project_local(normed):
+    all_fwd = lax.all_gather(normed_fwd, "seq", axis=0, tiled=True)
+    all_bwd = lax.all_gather(normed_bwd, "seq", axis=0, tiled=True)
+    all_grad = lax.all_gather(grad_low, "seq", axis=0, tiled=True)
+
+    def project(normed):
         query = rotate(
-            jnp.dot(normed, all_query, preferred_element_type=jnp.float32), local_cos, local_sin
+            jnp.dot(normed, w_query[0], preferred_element_type=jnp.float32), full_cos, full_sin
         ).astype(jnp.bfloat16)
         key_rows = rotate(
-            jnp.dot(normed, all_key, preferred_element_type=jnp.float32), local_cos, local_sin
+            jnp.dot(normed, w_key[0], preferred_element_type=jnp.float32), full_cos, full_sin
         ).astype(jnp.bfloat16)
-        value_rows = jnp.dot(normed, all_value, preferred_element_type=jnp.float32).astype(
+        value_rows = jnp.dot(normed, w_value[0], preferred_element_type=jnp.float32).astype(
             jnp.bfloat16
         )
-        return [query, key_rows, value_rows]
-
-    attn_grad = jnp.dot(grad_low, all_out, preferred_element_type=jnp.float32).astype(jnp.bfloat16)
-    pieces = jnp.stack(project_local(normed_fwd) + project_local(normed_bwd) + [attn_grad])
-    head_view = lax.all_to_all(pieces, "seq", split_axis=2, concat_axis=1, tiled=True)
-    attn = attend(head_view[0], head_view[1], head_view[2])
-    attn_tokens = to_tokens(attn[None])[0]
-    branch = times_t(attn_tokens, all_out)
+        return (query, key_rows, value_rows)
+
+    attn = attend(*project(all_fwd))
+    branch = lax.psum_scatter(
+        times_t(attn, w_out[0]).astype(jnp.bfloat16), "seq", scatter_dimension=0, tiled=True
+    )
+    attn_grad = jnp.dot(all_grad, w_out[0], preferred_element_type=jnp.float32).astype(jnp.bfloat16)
+    query_b, key_b, value_b = project(all_bwd)
     query_grad, key_grad, value_grad = attend_back(
-        head_view[3], head_view[4], head_view[5], head_view[6], full_cos, full_sin
-    )
-    grad_tokens = to_tokens(jnp.stack([query_grad, key_grad, value_grad]))
-    d_normed = (
-        times_t(grad_tokens[0], all_query)
-        + times_t(grad_tokens[1], all_key)
-        + times_t(grad_tokens[2], all_value)
-    )
-    act_out = act_in + branch
+        query_b, key_b, value_b, attn_grad, full_cos, full_sin
+    )
+    d_normed = lax.psum_scatter(
+        (
+            times_t(query_grad, w_query[0])
+            + times_t(key_grad, w_key[0])
+            + times_t(value_grad, w_value[0])
+        ).astype(jnp.bfloat16),
+        "seq",
+        scatter_dimension=0,
+        tiled=True,
+    ).astype(jnp.float32)
+    act_out = act_in + branch.astype(jnp.float32)
     gain_grad = d_normed * gain_row
     d_input = inv_bwd * gain_grad - saved_in * inv_bwd * inv_bwd * inv_bwd * jnp.mean(
         saved_in * gain_grad, -1, keepdims=True

time: 777 us -> 438 us (0.56); the launches traced: 763 us -> 437 us
  waiting for transfers between devices: 495 us -> 306 us
  local copies, waits for them, and re-layouts: 95 us -> 5.42 us
  matrix products: 111 us -> 90.4 us
  starting transfers between devices: 17.2 us -> 1.17 us
  other arithmetic: 29.8 us -> 19.9 us
    all_gather x4 -> x3, waiting for transfers between devices: 418 us -> 144 us  [the longest x1 66.6 us: shards(): all_bwd = lax.all_gather(normed_bwd, 'seq', axis=0, tiled=True)]
    reduce_scatter x0 -> x2, waiting for transfers between devices: none -> 152 us  [the longest x1 83.1 us: shards(): lax.psum_scatter(times_t(attn, w_out[0]).astype(jnp.bfloat16), 'seq', sca...]
    all_to_all x3 -> x0, waiting for transfers between devices: 70.1 us -> none  [the longest x1 56.7 us: shards(): lax.all_to_all(pieces, 'seq', split_axis=2, concat_axis=1, tiled=True)]
    dot_general x2, local copies, waits for them, and re-layouts: 24.8 us -> 2.84 us  [the longest x1 1.42 us: project(): jnp.dot(normed, w_key[0], preferred_element_type=jnp.float32)]
    another operation x6 -> x0, local copies, waits for them, and re-layouts: 18.3 us -> none  [the longest x4 8.3 us: split_heads(): return values.reshape(values.shape[0], -1, HD)]
    convert_element_type x7 -> x0, local copies, waits for them, and re-layouts: 16.2 us -> none  [the longest x1 3.58 us: attend_back(): rotate_back(query_grads.reshape(length, -1), cosine, sine_table)]
    all_to_all x3 -> x0, starting transfers between devices: 16.1 us -> none  [the longest x2 11.5 us: to_tokens(): lax.all_to_all(values, 'seq', split_axis=1, concat_axis=2, tiled=True)]
    dot_general x4, matrix products: 23.3 us -> 9.29 us  [times_t(): lax.dot_general(left, right, (((1,), (1,)), ((), ())), preferred_element_...]
  transfers between devices with their start and end apart: 9 -> 7, of which waited for: 7 -> 6; matrix products, arithmetic and copies ran while one was open for 17% -> 21% of each run, Pallas kernels for 0% -> 0%
where the time goes in v1:
time: 438 us; the launch traced here: 437 us
  waiting for transfers between devices  306 us (70%)
  matrix products  90.4 us (21%)
  other arithmetic  19.9 us (5%)
  between operations  14.1 us (3%)
  local copies, waits for them, and re-layouts  5.42 us (1%)
    reduce_scatter x1, waiting for transfers between devices, shards(): lax.psum_scatter(times_t(attn, w_out[0]).astype(jnp.bfloat16), 'seq', sca...  83.1 us
    reduce_scatter x1, waiting for transfers between devices, shards(): lax.psum_scatter((times_t(query_grad, w_query[0]) + times_t(key_grad, w_k...  68.6 us
    all_gather x1, waiting for transfers between devices, shards(): all_bwd = lax.all_gather(normed_bwd, 'seq', axis=0, tiled=True)  66.6 us
    all_gather x1, waiting for transfers between devices, shards(): all_grad = lax.all_gather(grad_low, 'seq', axis=0, tiled=True)  51.2 us
    all_gather x1, waiting for transfers between devices, shards(): all_fwd = lax.all_gather(normed_fwd, 'seq', axis=0, tiled=True)  26.3 us
    dot_general x1, matrix products, step(): jnp.einsum('hqk,qhd->khd', score_grad, query_block, preferred_element_typ...  15.4 us
    dot_general x1, matrix products, step(): jnp.einsum('hqk,khd->qhd', score_grad, key_heads, preferred_element_type=...  14.9 us
    ppermute x2, waiting for transfers between devices, passed_along(): return lax.ppermute(value, axis, pairs)  9.62 us
  transfers between devices with their start and end apart: 7, of which 6 were waited for; matrix products, arithmetic and copies ran while one was open for 21% of the time, Pallas kernels for 0%

profile of v1, /device:TPU:0, one launch (start us, length us, event | category | flops | bytes accessed | tf_op | source)
XLA Modules:
  0.0 437.1 jit_solution(6163161213774346154)
XLA Ops:
  7.2 1.5 fusion.53
  8.8 1.4 fusion.41
  10.2 2.8 multiply_convert_fusion.1
  13.0 0.0 all-gather.8.cloned.1.call-start
  13.0 2.1 bitcast_convert_fusion
  15.1 0.0 all-gather.4.cloned.1.call-start
  15.2 0.7 all-gather.4.cloned.1.call-update
  15.9 0.0 reduce-scatter.5.cloned.1.call-start
  15.9 1.4 copy.35
  17.4 1.4 copy.34
  18.8 1.8 multiply_cosine_fusion
  20.6 66.6 %all-gather.6.cloned.1.call-done = bf16[1024,2048]{1,0:T(8,128)(2,1)} async-done(((bf16[128,2048]{1,0:T(8,128)(2,1)}), bf16[1024,2048]{1,0:T(8,128)(2,1)}) %all-gather.6.cloned.1.call-update) | async-done | bytes 4194320 | tf_op jit(solution)/shard_map/all_gather | solution.py:146
  87.2 3.8 fusion.14
  91.0 3.8 fusion.12
  94.8 1.4 subtract_convert_fusion.2
  96.2 7.3 %fusion.79 = (f32[2,1024]{1,0:T(2,128)S(1)}, f32[2,1024,1024]{1,2,0:T(8,128)}) fusion(bf16[1024,2,64]{0,2,1:T(8,128)(2,1)} %get-tuple-element.38, bf16[1024,2,64]{0,2,1:T(8,128)(2,1)} %get-tuple-element.37, bf16[1024,2,64]{0,2,1:T(8,128)(2,1)} %get-tuple-element.59, bf16[1024,2,64]{0,2,1:T(8,128)(2,1)} %get-tuple-element.60), kind=kOutput, calls=%fused_computation.107 | convolution fusion | flops 545260544 | bytes 9445376 | tf_op jit(solution)/shard_map/while/body/eval_jaxpr/sub | solution.py:103
  103.4 4.3 convolution_convert_fusion.1
  107.7 51.2 %all-gather.8.cloned.1.call-done = bf16[1024,2048]{1,0:T(8,128)(2,1)} async-done(((bf16[128,2048]{1,0:T(8,128)(2,1)}), bf16[1024,2048]{1,0:T(8,128)(2,1)}) %all-gather.8.cloned.1.call-update) | async-done | bytes 4194320 | tf_op jit(solution)/shard_map/all_gather | solution.py:147
  159.0 3.8 convolution_convert_fusion.2
  162.8 0.8 copy-done.11
  163.6 4.5 %fusion.81 = f32[2,1024,1024]{1,2,0:T(8,128)} fusion(bf16[1024,2,128]{0,2,1:T(8,128)(2,1)S(1)} %bitcast.110, bf16[1024,2,128]{0,2,1:T(8,128)(2,1)S(1)} %bitcast.112), kind=kOutput, calls=%fused_computation.109 | convolution fusion | flops 536870912 | bytes 9437184 | tf_op jit(solution)/shard_map/while/body/eval_jaxpr/qhd,khd->hqk/dot_general | solution.py:110
  168.2 15.4 %fusion.34 = f32[1024,2,128]{0,2,1:T(8,128)} fusion(f32[2,1024,1024]{1,2,0:T(8,128)} %fusion.81, bf16[1024,2,64]{0,2,1:T(8,128)(2,1)} %get-tuple-element.38, bf16[1024,2,64]{0,2,1:T(8,128)(2,1)} %get-tuple-element.37, f32[2,1024,1024]{1,2,0:T(8,128)} %get-tuple-element.66, f32[2,1024]{1,0:T(2,128)S(1)} %get-tuple-element.65), kind=kOutput, calls=%fused_computation.32 | convolution fusion | flops 552602624 | bytes 18358272 | tf_op jit(solution)/shard_map/while/body/eval_jaxpr/hqk,qhd->khd/dot_general | solution.py:118
  183.6 14.9 %fusion.31 = f32[1024,2,128]{0,2,1:T(8,128)} fusion(f32[2,1024,1024]{1,2,0:T(8,128)} %fusion.81, bf16[1024,2,64]{0,2,1:T(8,128)(2,1)} %get-tuple-element.59, bf16[1024,2,64]{0,2,1:T(8,128)(2,1)} %get-tuple-element.60, f32[2,1024,1024]{1,2,0:T(8,128)} %get-tuple-element.66, f32[2,1024]{1,0:T(2,128)S(1)} %get-tuple-element.65), kind=kOutput, calls=%fused_computation.31 | convolution fusion | flops 552602624 | bytes 18358272 | tf_op jit(solution)/shard_map/while/body/eval_jaxpr/hqk,khd->qhd/dot_general | solution.py:115
  198.5 5.9 %fusion.38 = bf16[2,128,1024]{2,1,0:T(8,128)(2,1)} fusion(bf16[1024,2,128]{0,2,1:T(8,128)(2,1)} %bitcast.111, f32[2,1024,1024]{1,2,0:T(8,128)} %get-tuple-element.66, f32[2,1024]{1,0:T(2,128)S(1)} %get-tuple-element.65), kind=kOutput, calls=%fused_computation.34 | convolution fusion | flops 541327360 | bytes 9445376 | tf_op jit(solution)/shard_map/while/body/eval_jaxpr/hqk,qhd->khd/dot_general | solution.py:104
  204.4 26.3 %all-gather.4.cloned.1.call-done = bf16[1024,2048]{1,0:T(8,128)(2,1)} async-done(((bf16[128,2048]{1,0:T(8,128)(2,1)}), bf16[1024,2048]{1,0:T(8,128)(2,1)}) %all-gather.4.cloned.1.call-update) | async-done | bytes 4194320 | tf_op jit(solution)/shard_map/all_gather | solution.py:145
  230.7 3.9 fusion.16
  234.6 3.8 fusion.18
  238.4 1.7 add_convert_fusion.1
  240.2 1.3 fusion.48
  241.6 1.3 fusion.46
  243.0 3.4 add_convert_fusion
  246.4 0.0 reduce-scatter.3.cloned.1.call-start
  246.5 5.2 %fusion.80 = (f32[2,1024]{1,0:T(2,128)S(1)}, f32[2,1024,1024]{1,2,0:T(8,128)}) fusion(bf16[1024,2,64]{0,2,1:T(8,128)(2,1)S(1)} %copy-done.13, bf16[1024,2,64]{0,2,1:T(8,128)(2,1)S(1)} %copy-done.14, bf16[1024,2,64]{0,2,1:T(8,128)(2,1)S(1)} %copy-done.15, bf16[1024,2,64]{0,2,1:T(8,128)(2,1)S(1)} %copy-done.16), kind=kOutput, calls=%fused_computation.108 | convolution fusion | flops 545260544 | bytes 9445376 | tf_op jit(solution)/shard_map/while/body/eval_jaxpr/sub | solution.py:77
  251.7 3.8 convolution_convert_fusion.3
  255.4 1.3 copy-done.18
  256.7 0.7 fusion.37
  257.5 0.5 copy-done.7
  257.9 3.3 convolution_convert_fusion
  261.2 68.6 %reduce-scatter.5.cloned.1.call-done = bf16[128,2048]{1,0:T(8,128)(2,1)} async-done(((bf16[1024,2048]{1,0:T(8,128)(2,1)}), bf16[128,2048]{1,0:T(8,128)(2,1)}) %reduce-scatter.5.cloned.1.call-update) | async-done | bytes 524304 | tf_op jit(solution)/shard_map/reduce_scatter | solution.py:170
  329.8 1.3 fusion.42
  331.0 2.5 fusion.43
  333.6 0.9 collective-permute-start.1
  334.4 83.1 %reduce-scatter.3.cloned.1.call-done = bf16[128,2048]{1,0:T(8,128)(2,1)} async-done(((bf16[1024,2048]{1,0:T(8,128)(2,1)}), bf16[128,2048]{1,0:T(8,128)(2,1)}) %reduce-scatter.3.cloned.1.call-update) | async-done | bytes 524304 | tf_op jit(solution)/shard_map/reduce_scatter | solution.py:162
  417.6 1.1 fusion.56
  418.7 0.1 collective-permute-start
  418.8 1.1 bitcast_convert_fusion.1
  419.9 9.6 %collective-permute-done = bf16[128,2048]{1,0:T(8,128)(2,1)S(1)} collective-permute-done((bf16[128,2048]{1,0:T(8,128)(2,1)S(1)}, bf16[128,2048]{1,0:T(8,128)(2,1)S(1)}, u32[]{:S(2)}, u32[]{:S(2)}) %collective-permute-start) | collective-permute-done | bytes 524320 | tf_op jit(solution)/shard_map/ppermute | solution.py:12
  429.5 1.1 bitcast_convert_fusion.2
  (47 shorter events, 0.3 us)
Async XLA Ops:
  7.2 96.3 %copy-start = (bf16[1,2048,256]{2,1,0:T(8,128)(2,1)S(1)}, bf16[1,2048,256]{2,1,0:T(8,128)(2,1)}, u32[]{:S(2)}) copy-start(bf16[1,2048,256]{2,1,0:T(8,128)(2,1)} %param.14) | copy-start | bytes 3145732
  7.2 8.8 %copy-start.4 = (bf16[1,2048,256]{2,1,0:T(8,128)(2,1)S(1)}, bf16[1,2048,256]{2,1,0:T(8,128)(2,1)}, u32[]{:S(2)}) copy-start(bf16[1,2048,256]{2,1,0:T(8,128)(2,1)} %param.13) | copy-start | bytes 3145732
  7.2 10.2 %copy-start.3 = (bf16[1,2048,256]{2,1,0:T(8,128)(2,1)S(1)}, bf16[1,2048,256]{2,1,0:T(8,128)(2,1)}, u32[]{:S(2)}) copy-start(bf16[1,2048,256]{2,1,0:T(8,128)(2,1)} %param.12) | copy-start | bytes 3145732
  7.2 80.0 %all-gather.6.cloned.1.call-start = ((), (), s32[]{:S(2)}) async-start(), calls=%async_computation.4 | async-start | bytes 4718592 | tf_op jit(solution)/shard_map/all_gather | solution.py:146
  13.0 146.0 %all-gather.8.cloned.1.call-start = ((), (), s32[]{:S(2)}) async-start(), calls=%async_computation.5 | async-start | bytes 4718592 | tf_op jit(solution)/shard_map/all_gather | solution.py:147
  15.1 215.6 %all-gather.4.cloned.1.call-start = ((), (), s32[]{:S(2)}) async-start(), calls=%async_computation.2 | async-start | bytes 4718592 | tf_op jit(solution)/shard_map/all_gather | solution.py:145
  15.9 313.9 %reduce-scatter.5.cloned.1.call-start = ((), (), s32[]{:S(2)}) async-start(), calls=%async_computation.6 | async-start | bytes 4718592 | tf_op jit(solution)/shard_map/reduce_scatter | solution.py:170
  87.2 7.6 %copy-start.5 = (f32[1024,64]{0,1:T(8,128)S(1)}, f32[1024,64]{0,1:T(8,128)}, u32[]{:S(2)}) copy-start(f32[1024,64]{0,1:T(8,128)} %get-tuple-element.64) | copy-start | bytes 786436
  159.0 4.6 %copy-start.12 = (bf16[1024,256]{0,1:T(8,128)(2,1)S(1)}, bf16[1024,256]{0,1:T(8,128)(2,1)}, u32[]{:S(2)}) copy-start(bf16[1024,256]{0,1:T(8,128)(2,1)} %convolution_convert_fusion.1) | copy-start | bytes 1572868
  162.8 0.8 copy-start.11
  230.7 7.7 %copy-start.6 = (f32[1024,64]{0,1:T(8,128)S(1)}, f32[1024,64]{0,1:T(8,128)}, u32[]{:S(2)}) copy-start(f32[1024,64]{0,1:T(8,128)} %get-tuple-element.64) | copy-start | bytes 786436
  230.7 7.7 %copy-start.8 = (f32[1024,2,128]{0,2,1:T(8,128)S(1)}, f32[1024,2,128]{0,2,1:T(8,128)}, u32[]{:S(2)}) copy-start(f32[1024,2,128]{0,2,1:T(8,128)} %fusion.34) | copy-start | bytes 3145732
  230.7 7.7 %copy-start.9 = (f32[1024,2,128]{0,2,1:T(8,128)S(1)}, f32[1024,2,128]{0,2,1:T(8,128)}, u32[]{:S(2)}) copy-start(f32[1024,2,128]{0,2,1:T(8,128)} %fusion.31) | copy-start | bytes 3145732
  241.5 1.4 copy-start.10
  242.9 3.5 copy-start.13
  242.9 3.5 copy-start.14
  242.9 3.5 copy-start.15
  243.0 3.5 copy-start.16
  246.4 171.2 %reduce-scatter.3.cloned.1.call-start = ((), (), s32[]{:S(2)}) async-start(), calls=%async_computation.3 | async-start | bytes 4718592 | tf_op jit(solution)/shard_map/reduce_scatter | solution.py:162
  251.7 5.0 %copy-start.18 = (f32[2,1024,1024]{1,2,0:T(8,128)S(1)}, f32[2,1024,1024]{1,2,0:T(8,128)}, u32[]{:S(2)}) copy-start(f32[2,1024,1024]{1,2,0:T(8,128)} %get-tuple-element.68) | copy-start | bytes 25165828
  256.7 1.2 copy-start.7
  257.4 72.3 %copy-start.1 = (f32[1,128,2048]{2,1,0:T(8,128)S(1)}, f32[1,128,2048]{2,1,0:T(8,128)}, u32[]{:S(2)}) copy-start(f32[1,128,2048]{2,1,0:T(8,128)} %param.9) | copy-start | bytes 3145732
  257.4 72.3 %copy-start.17 = (f32[1,2048]{1,0:T(1,128)S(1)}, f32[1,2048]{1,0:T(1,128)}, u32[]{:S(2)}) copy-start(f32[1,2048]{1,0:T(1,128)} %param.11) | copy-start | bytes 24580
  257.9 159.7 %copy-start.2 = (f32[1,128,2048]{2,1,0:T(8,128)S(1)}, f32[1,128,2048]{2,1,0:T(8,128)}, u32[]{:S(2)}) copy-start(f32[1,128,2048]{2,1,0:T(8,128)} %param.8) | copy-start | bytes 3145732
  333.6 85.3 %collective-permute-start.1 = (bf16[128,2048]{1,0:T(8,128)(2,1)}, bf16[128,2048]{1,0:T(8,128)(2,1)S(1)}, u32[]{:S(2)}, u32[]{:S(2)}) collective-permute-start(bf16[128,2048]{1,0:T(8,128)(2,1)} %fusion.43), channel_id=1, source_target_pairs={{0,120},{8,0},{16,8},{24,16},{32,24},{40,32},{48,40},{56,48},{64,5... | collective-permute-start | bytes 1572872 | tf_op jit(solution)/shard_map/ppermute | solution.py:12
  418.7 10.8 %collective-permute-start = (bf16[128,2048]{1,0:T(8,128)(2,1)S(1)}, bf16[128,2048]{1,0:T(8,128)(2,1)S(1)}, u32[]{:S(2)}, u32[]{:S(2)}) collective-permute-start(bf16[128,2048]{1,0:T(8,128)(2,1)S(1)} %fusion.56), channel_id=1, source_target_pairs={{0,8},{8,16},{16,24},{24,32},{32,40},{40,48},{48,56},{56,64},{64,7... | collective-permute-start | bytes 1572872 | tf_op jit(solution)/shard_map/ppermute | solution.py:12
Sparse Core Ops, SparseCore 0:
  13.1 74.0 all-gather.5
  89.5 69.4 all-gather.7
  161.3 69.3 all-gather.3
  246.5 83.1 reduce-scatter.4
  333.5 84.0 reduce-scatter.2

commit v2 on v1

v2 whole, which is shorter than its diff:
```python
import math

import jax
import jax.numpy as jnp
import numpy as np
from jax import lax
from jax.experimental import pallas as pl
from jax.experimental.pallas import tpu as pltpu
from jax.sharding import PartitionSpec as P

HD = 128
MESH = pl.DeviceIdType.MESH
F32 = jnp.float32
BF16 = jnp.bfloat16
SCALE = HD ** (-0.5)
LOG2E = math.log2(math.e)


def rope_constants(length):
    inverse = 10000.0 ** (-(np.arange(HD // 2, dtype=np.float64) * 2.0 / HD))
    angles = np.arange(length, dtype=np.float64)[:, None] * inverse[None, :]
    cosine, sine = np.cos(angles), np.sin(angles)
    return (
        np.concatenate([cosine, cosine], 1).astype(np.float32),
        np.concatenate([-sine, sine], 1).astype(np.float32),
    )


def dot_nn(left, right):
    return jnp.dot(left, right, preferred_element_type=F32)


def dot_nt(left, right):
    return lax.dot_general(left, right, (((1,), (1,)), ((), ())), preferred_element_type=F32)


def kernel(
    x_fwd_hbm,
    x_bwd_hbm,
    grad_hbm,
    gain_ref,
    wq_hbm,
    wk_hbm,
    wv_hbm,
    wo_hbm,
    cos_hbm,
    sin_hbm,
    act_ref,
    dgrad_ref,
    x_fwd,
    x_bwd,
    grad,
    wq,
    wk,
    wv,
    wo,
    cos,
    sin,
    w3t,
    wot,
    gat_f,
    gat_b,
    gat_g,
    q_ref,
    k_ref,
    v_ref,
    g_ref,
    kt_ref,
    vt_ref,
    dk_acc,
    dv_acc,
    dqkv,
    attn,
    part_b,
    part_f,
    recv_b,
    recv_f,
    out_b,
    out_f,
    load_sem,
    send_sem,
    recv_sem,
):
    rows = x_fwd.shape[0]
    half, quarter = rows // 2, rows // 4
    length, width = gat_f.shape
    feats = wq.shape[1]
    heads = feats // HD
    pipe, seq = lax.axis_index("pipe"), lax.axis_index("seq")
    n_pipe = lax.axis_size("pipe")
    n_x = lax.axis_size("seq") // 2
    my_x, my_y = lax.div(seq, 2), lax.rem(seq, 2)
    left_x, right_x, far_x = (lax.rem(my_x + step, n_x) for step in (n_x - 1, 1, 2))
    own_row, other_row = my_y, 1 - my_y

    def slot(x, y):
        return x * 2 + y

    def at(x, y, start, count):
        return pl.ds(pl.multiple_of(slot(x, y) * rows + start, 32), count)

    devices = {
        "L": (pipe, slot(left_x, my_y)),
        "R": (pipe, slot(right_x, my_y)),
        "Y": (pipe, slot(my_x, 1 - my_y)),
        "N": (lax.rem(pipe + 1, n_pipe), seq),
        "P": (lax.rem(pipe + n_pipe - 1, n_pipe), seq),
    }

    loads = {}

    def load(index, src, dst):
        loads[index] = pltpu.make_async_copy(src, dst, load_sem.at[index])
        loads[index].start()

    load(0, x_bwd_hbm, x_bwd)
    load(1, grad_hbm, grad)
    load(2, x_fwd_hbm, x_fwd)
    load(3, wq_hbm, wq)
    load(4, wk_hbm, wk)
    load(5, wv_hbm, wv)
    load(6, wo_hbm, wo)
    load(7, cos_hbm, cos)
    load(8, sin_hbm, sin)

    barrier = pltpu.get_barrier_semaphore()
    for device in devices.values():
        pl.semaphore_signal(barrier, inc=1, device_id=device, device_id_type=MESH)

    copies = {}

    def describe(name):
        index, refs, where = copies[name]
        src, dst = refs()
        return pltpu.make_async_remote_copy(
            src_ref=src,
            dst_ref=dst,
            send_sem=send_sem.at[index],
            recv_sem=recv_sem.at[index],
            device_id=devices[where],
            device_id_type=MESH,
        )

    def send(name, refs, where):
        copies[name] = (len(copies), refs, where)
        describe(name).start()

    def arrived(name):
        describe(name).wait_recv()

    def normalize_into(source, target):
        def body(i, carry):
            here = pl.ds(pl.multiple_of(i * quarter, quarter), quarter)
            values = source[here, :]
            inv_rms = lax.rsqrt(jnp.mean(values * values, -1, keepdims=True) + 1e-05)
            there = at(my_x, my_y, i * quarter, quarter)
            target[there, :] = (values * inv_rms * gain_ref[...]).astype(BF16)
            return carry

        lax.fori_loop(0, rows // quarter, body, 0)

    def round_into(source, target):
        def body(i, carry):
            here = pl.ds(pl.multiple_of(i * quarter, quarter), quarter)
            target[at(my_x, my_y, i * quarter, quarter), :] = source[here, :].astype(BF16)
            return carry

        lax.fori_loop(0, rows // quarter, body, 0)

    def pass_on(tag, buf, x, y, start, count, where):
        send(tag + where, lambda: (buf.at[at(x, y, start, count)],) * 2, where)

    def gather_start(tag, buf):
        pass_on(tag + "a0", buf, my_x, my_y, 0, half, "Y")
        for where in "LR":
            pass_on(tag + "a0", buf, my_x, my_y, 0, half, where)
        for where in "LRY":
            pass_on(tag + "b0", buf, my_x, my_y, half, half, where)

    def gather_near_a(tag, buf):
        arrived(tag + "a0R")
        pass_on(tag + "a1", buf, left_x, my_y, 0, quarter, "R")
        arrived(tag + "a0L")
        pass_on(tag + "a1", buf, right_x, my_y, quarter, quarter, "L")

    def gather_cross_a(tag, buf):
        arrived(tag + "a0Y")
        for where in "LR":
            pass_on(tag + "a2", buf, my_x, other_row, 0, half, where)

    def gather_near_b(tag, buf):
        arrived(tag + "b0R")
        pass_on(tag + "b1", buf, left_x, my_y, half, quarter, "R")
        pass_on(tag + "b1l", buf, left_x, my_y, half, half, "Y")
        arrived(tag + "b0L")
        pass_on(tag + "b1", buf, right_x, my_y, half + quarter, quarter, "L")
        pass_on(tag + "b1r", buf, right_x, my_y, half, half, "Y")

    def gather_far_b(tag, buf):
        arrived(tag + "b1R")
        pass_on(tag + "b2r", buf, far_x, my_y, half, quarter, "Y")
        arrived(tag + "b1L")
        pass_on(tag + "b2l", buf, far_x, my_y, half + quarter, quarter, "Y")

    def gather_far_a(tag, buf):
        arrived(tag + "a2R")
        pass_on(tag + "a3", buf, left_x, other_row, 0, quarter, "R")
        arrived(tag + "a2L")
        pass_on(tag + "a3", buf, right_x, other_row, quarter, quarter, "L")

    def gather_end(tag, buf):
        for name in ("a1R", "a1L", "b0Y", "b1lY", "b1rY", "a3R", "a3L", "b2rY", "b2lY"):
            arrived(tag + name)

    places = {}
    cursor = 0
    for name, count in (
        ("a0R0", quarter),
        ("a0L0", quarter),
        ("a0R1", quarter),
        ("a0L1", quarter),
        ("a1R0", half),
        ("a1L0", half),
        ("a1R1", half),
        ("a1L1", half),
        ("a2Y", half),
        ("b0Yf", half),
        ("b0Yr", half),
        ("b0Yl", half),
        ("b0Ym", half),
        ("b1R", quarter),
        ("b1L", quarter),
        ("b2R", half),
        ("b2L", half),
    ):
        places[name] = pl.ds(cursor, count)
        cursor += count

    def to(tag, name, part, recv, x, y, start, count, where):
        send(
            tag + name, lambda: (part.at[at(x, y, start, count)], recv.at[places[name]]), where
        )

    def add_in(part, recv, name, x, y, start, count):
        here = at(x, y, start, count)
        part[here, :] = (part[here, :].astype(F32) + recv[places[name], :].astype(F32)).astype(BF16)

    def reduce_far(tag, part, recv):
        for w, y in ((1, other_row), (0, own_row)):
            to(tag, f"a0R{w}", part, recv, far_x, y, 0, quarter, "R")
            to(tag, f"a0L{w}", part, recv, far_x, y, quarter, quarter, "L")
        to(tag, "b0Yf", part, recv, far_x, other_row, half, half, "Y")

    def reduce_cross(tag, part, recv, x, name):
        to(tag, name, part, recv, x, other_row, half, half, "Y")

    def reduce_near_a(tag, part, recv):
        for w, y in ((1, other_row), (0, own_row)):
            arrived(tag + f"a0R{w}")
            add_in(part, recv, f"a0R{w}", right_x, y, 0, quarter)
            to(tag, f"a1R{w}", part, recv, right_x, y, 0, half, "R")
            arrived(tag + f"a0L{w}")
            add_in(part, recv, f"a0L{w}", left_x, y, quarter, quarter)
            to(tag, f"a1L{w}", part, recv, left_x, y, 0, half, "L")

    def reduce_far_b(tag, part, recv):
        arrived(tag + "b0Yf")
        add_in(part, recv, "b0Yf", far_x, own_row, half, half)
        to(tag, "b1R", part, recv, far_x, own_row, half, quarter, "R")
        to(tag, "b1L", part, recv, far_x, own_row, half + quarter, quarter, "L")
        arrived(tag + "b0Yr")
        add_in(part, recv, "b0Yr", right_x, own_row, half, half)
        arrived(tag + "b0Yl")
        add_in(part, recv, "b0Yl", left_x, own_row, half, half)

    def reduce_cross_a(tag, part, recv):
        arrived(tag + "a1R1")
        arrived(tag + "a1L1")
        add_in(part, recv, "a1R1", my_x, other_row, 0, half)
        add_in(part, recv, "a1L1", my_x, other_row, 0, half)
        to(tag, "a2Y", part, recv, my_x, other_row, 0, half, "Y")

    def reduce_near_b(tag, part, recv):
        arrived(tag + "b1R")
        add_in(part, recv, "b1R", right_x, own_row, half, quarter)
        to(tag, "b2R", part, recv, right_x, own_row, half, half, "R")
        arrived(tag + "b1L")
        add_in(part, recv, "b1L", left_x, own_row, half + quarter, quarter)
        to(tag, "b2L", part, recv, left_x, own_row, half, half, "L")

    def last_a(tag):
        for name in ("a1R0", "a1L0", "a2Y"):
            arrived(tag + name)
        return ("a1R0", "a1L0", "a2Y")

    def last_b(tag):
        for name in ("b2R", "b2L", "b0Ym"):
            arrived(tag + name)
        return ("b2R", "b2L", "b0Ym")

    step_rows = 16

    def total_of(part, recv, names, start, i):
        offset = pl.multiple_of(i * step_rows, step_rows)
        here = pl.ds(pl.multiple_of(slot(my_x, my_y) * rows + start + offset, step_rows), step_rows)
        total = part[here, :].astype(F32)
        for name in names:
            total += recv[pl.ds(places[name].start + offset, step_rows), :].astype(F32)
        return total

    def finish_act(part, recv, names, start, name):
        def body(i, carry):
            here = pl.ds(start + pl.multiple_of(i * step_rows, step_rows), step_rows)
            out_f[here, :] = (x_fwd[here, :] + total_of(part, recv, names, start, i)).astype(BF16)
            return carry

        lax.fori_loop(0, half // step_rows, body, 0)
        send(name, lambda: (out_f.at[pl.ds(start, half)], act_ref.at[pl.ds(start, half)]), "N")

    def finish_grad(part, recv, names, start, name):
        def body(i, carry):
            here = pl.ds(start + pl.multiple_of(i * step_rows, step_rows), step_rows)
            saved = x_bwd[here, :]
            inv_rms = lax.rsqrt(jnp.mean(saved * saved, -1, keepdims=True) + 1e-05)
            gain_grad = total_of(part, recv, names, start, i) * gain_ref[...]
            mean = jnp.mean(saved * gain_grad, -1, keepdims=True)
            d_input = inv_rms * gain_grad - saved * (inv_rms * inv_rms * inv_rms * mean)
            out_b[here, :] = (grad[here, :] + d_input).astype(BF16)
            return carry

        lax.fori_loop(0, half // step_rows, body, 0)
        send(name, lambda: (out_b.at[pl.ds(start, half)], dgrad_ref.at[pl.ds(start, half)]), "P")

    block = 256
    blocks = length // block

    def rotated(values, here, sign):
        out = values * cos[here, :]
        turned = pltpu.roll(values, HD // 2, 1) * sin[here, :]
        return out + turned if sign > 0 else out - turned

    def project(buf):
        def body(i, carry):
            here = pl.ds(pl.multiple_of(i * block, block), block)
            normed = buf[here, :]
            query = dot_nn(normed, wq[...])
            key = dot_nn(normed, wk[...])
            for h in range(heads):
                head = slice(h * HD, (h + 1) * HD)
                q_ref[here, head] = rotated(query[:, head], here, 1).astype(BF16)
                turned = rotated(key[:, head], here, 1)
                k_ref[here, head] = turned.astype(BF16)
                kt_ref[head, here] = turned.T.astype(BF16)
            value = dot_nn(normed, wv[...])
            v_ref[here, :] = value.astype(BF16)
            vt_ref[:, here] = value.T.astype(BF16)
            return carry

        lax.fori_loop(0, blocks, body, 0)

    def project_grad(buf):
        def body(i, carry):
            here = pl.ds(pl.multiple_of(i * block, block), block)
            g_ref[here, :] = dot_nn(buf[here, :], wo[...]).astype(BF16)
            return carry

        lax.fori_loop(0, blocks, body, 0)

    def run_actions(actions, h, i):
        for number, todo in actions.items():
            if number // blocks == h:

                @pl.when(i == number % blocks)
                def _(todo=todo):
                    for act in todo:
                        act()

    def exponentials(h, here):
        head = slice(h * HD, (h + 1) * HD)
        scores = dot_nt(k_ref[:, head], q_ref[here, head])
        top = jnp.max(scores, axis=0, keepdims=True)
        weights = jnp.exp2((scores - top) * (SCALE * LOG2E))
        return weights, 1.0 / jnp.sum(weights, axis=0, keepdims=True)

    def attend_back(actions):
        for h in range(heads):
            head = slice(h * HD, (h + 1) * HD)
            dk_acc[...] = jnp.zeros_like(dk_acc)
            dv_acc[...] = jnp.zeros_like(dv_acc)

            def body(i, carry, h=h, head=head):
                run_actions(actions, h, i)
                here = pl.ds(pl.multiple_of(i * block, block), block)
                weights, inverse = exponentials(h, here)
                probs = weights * inverse
                d_out = g_ref[here, head]
                dv_acc[...] += dot_nn(probs.astype(BF16), d_out)
                d_probs = dot_nt(v_ref[:, head], d_out)
                delta = jnp.sum(probs * d_probs, axis=0, keepdims=True)
                d_scores = (probs * (d_probs - delta) * SCALE).astype(BF16)
                dk_acc[...] += dot_nn(d_scores, q_ref[here, head])
                d_query = dot_nn(kt_ref[head, :], d_scores).T
                dqkv[here, head] = rotated(d_query, here, -1).astype(BF16)
                return carry

            lax.fori_loop(0, blocks, body, 0)

            def close(i, carry, h=h):
                here = pl.ds(pl.multiple_of(i * block, block), block)
                d_key = rotated(dk_acc[here, :], here, -1)
                dqkv[here, feats + h * HD : feats + (h + 1) * HD] = d_key.astype(BF16)
                dqkv[here, 2 * feats + h * HD : 2 * feats + (h + 1) * HD] = dv_acc[here, :].astype(BF16)
                return carry

            lax.fori_loop(0, blocks, close, 0)

    def attend(actions):
        for h in range(heads):
            head = slice(h * HD, (h + 1) * HD)

            def body(i, carry, h=h, head=head):
                run_actions(actions, h, i)
                here = pl.ds(pl.multiple_of(i * block, block), block)
                weights, inverse = exponentials(h, here)
                out = dot_nn(vt_ref[head, :], weights.astype(BF16)) * inverse
                attn[here, head] = out.T.astype(BF16)
                return carry

            lax.fori_loop(0, blocks, body, 0)

    columns = 512

    def multiply_out(source, weights, part, x):
        here = pl.ds(pl.multiple_of(x * block, block), block)

        def body(i, carry):
            there = pl.ds(pl.multiple_of(i * columns, columns), columns)
            part[here, there] = dot_nn(source[here, :], weights[:, there]).astype(BF16)
            return carry

        lax.fori_loop(0, width // columns, body, 0)

    def transpose_into(source, target, offset):
        def body(i, carry):
            here = pl.ds(pl.multiple_of(i * feats, feats), feats)
            target[offset : offset + feats, here] = source[here, :].T
            return carry

        lax.fori_loop(0, width // feats, body, 0)

    loads[0].wait()
    normalize_into(x_bwd, gat_b)
    pl.semaphore_wait(barrier, len(devices))
    gather_start("B", gat_b)
    loads[1].wait()
    round_into(grad, gat_g)
    loads[2].wait()
    normalize_into(x_fwd, gat_f)
    gather_near_a("B", gat_b)
    gather_cross_a("B", gat_b)
    for index in range(3, 9):
        loads[index].wait()
    gather_start("G", gat_g)
    transpose_into(wq, w3t, 0)
    gather_near_b("B", gat_b)
    gather_far_b("B", gat_b)
    transpose_into(wk, w3t, feats)
    gather_far_a("B", gat_b)
    transpose_into(wv, w3t, 2 * feats)
    transpose_into(wo, wot, 0)
    gather_near_a("G", gat_g)
    gather_cross_a("G", gat_g)
    gather_near_b("G", gat_g)
    gather_far_b("G", gat_g)
    gather_start("F", gat_f)
    gather_end("B", gat_b)
    project(gat_b)
    gather_far_a("G", gat_g)
    gather_end("G", gat_g)
    project_grad(gat_g)
    attend_back(
        {
            0: [lambda: gather_near_a("F", gat_f)],
            1: [lambda: gather_cross_a("F", gat_f)],
            3: [lambda: gather_near_b("F", gat_f)],
            4: [lambda: gather_far_b("F", gat_f)],
            6: [lambda: gather_far_a("F", gat_f)],
        }
    )
    gather_end("F", gat_f)

    multiply_out(dqkv, w3t, part_b, far_x)
    reduce_far("RB", part_b, recv_b)
    multiply_out(dqkv, w3t, part_b, right_x)
    reduce_cross("RB", part_b, recv_b, right_x, "b0Yr")
    multiply_out(dqkv, w3t, part_b, left_x)
    reduce_cross("RB", part_b, recv_b, left_x, "b0Yl")
    multiply_out(dqkv, w3t, part_b, my_x)
    reduce_cross("RB", part_b, recv_b, my_x, "b0Ym")
    reduce_near_a("RB", part_b, recv_b)
    project(gat_f)
    reduce_far_b("RB", part_b, recv_b)
    attend(
        {
            2: [lambda: reduce_cross_a("RB", part_b, recv_b)],
            4: [lambda: reduce_near_b("RB", part_b, recv_b)],
        }
    )

    multiply_out(attn, wot, part_f, far_x)
    reduce_far("RF", part_f, recv_f)
    multiply_out(attn, wot, part_f, right_x)
    reduce_cross("RF", part_f, recv_f, right_x, "b0Yr")
    multiply_out(attn, wot, part_f, left_x)
    reduce_cross("RF", part_f, recv_f, left_x, "b0Yl")
    multiply_out(attn, wot, part_f, my_x)
    reduce_cross("RF", part_f, recv_f, my_x, "b0Ym")
    finish_grad(part_b, recv_b, last_a("RB"), 0, "PBa")
    reduce_near_a("RF", part_f, recv_f)
    finish_grad(part_b, recv_b, last_b("RB"), half, "PBb")
    reduce_far_b("RF", part_f, recv_f)
    reduce_cross_a("RF", part_f, recv_f)
    reduce_near_b("RF", part_f, recv_f)
    finish_act(part_f, recv_f, last_a("RF"), 0, "PFa")
    finish_act(part_f, recv_f, last_b("RF"), half, "PFb")
    for name in ("PBa", "PBb", "PFa", "PFb"):
        arrived(name)
    for name in copies:
        describe(name).wait_send()


def shards(x_fwd, x_bwd, grad_in, gain, w_query, w_key, w_value, w_out):
    rows, width = x_fwd.shape[1:]
    feats = w_query.shape[2]
    length = rows * lax.axis_size("seq")
    cosine, sine = (jnp.asarray(table) for table in rope_constants(length))
    anywhere = pl.BlockSpec(memory_space=pl.ANY)
    vmem = pltpu.VMEM
    recv_rows = rows * 7
    n_copies = 96
    act, dgrad = pl.pallas_call(
        kernel,
        out_shape=[jax.ShapeDtypeStruct((rows, width), BF16)] * 2,
        in_specs=[anywhere] * 3 + [pl.BlockSpec(memory_space=pltpu.VMEM)] + [anywhere] * 6,
        out_specs=[anywhere] * 2,
        scratch_shapes=[vmem((rows, width), F32)] * 3
        + [vmem((width, feats), BF16)] * 4
        + [vmem((length, HD), F32)] * 2
        + [vmem((3 * feats, width), BF16), vmem((feats, width), BF16)]
        + [vmem((length, width), BF16)] * 3
        + [vmem((length, feats), BF16)] * 4
        + [vmem((feats, length), BF16)] * 2
        + [vmem((length, HD), F32)] * 2
        + [vmem((length, 3 * feats), BF16), vmem((length, feats), BF16)]
        + [vmem((length, width), BF16)] * 2
        + [vmem((recv_rows, width), BF16)] * 2
        + [vmem((rows, width), BF16)] * 2
        + [
            pltpu.SemaphoreType.DMA((9,)),
            pltpu.SemaphoreType.DMA((n_copies,)),
            pltpu.SemaphoreType.DMA((n_copies,)),
        ],
        compiler_params=pltpu.CompilerParams(
            collective_id=0, has_side_effects=True, vmem_limit_bytes=67_043_328
        ),
        name="relay_attention",
    )(
        x_fwd[0],
        x_bwd[0],
        grad_in[0],
        gain,
        w_query[0],
        w_key[0],
        w_value[0],
        w_out[0],
        cosine,
        sine,
    )
    return (act.astype(F32)[None], dgrad.astype(F32)[None])


def solution(mesh):
    placed = (
        P("pipe", "seq", None),
        P("pipe", "seq", None),
        P("pipe", "seq", None),
        P("pipe", None),
        P("pipe", None, "seq"),
        P("pipe", None, "seq"),
        P("pipe", None, "seq"),
        P("pipe", None, "seq"),
    )
    return jax.shard_map(
        shards,
        mesh=mesh,
        in_specs=placed,
        out_specs=(P("pipe", "seq", None), P("pipe", "seq", None)),
        check_vma=False,
    )
```

time: 438 us -> 168 us (0.38)
  waiting for transfers between devices: 306 us -> 0 us
  Pallas kernels: 0 us -> 165 us
  matrix products: 90.4 us -> 0 us
  other arithmetic: 19.9 us -> 2.76 us
  between operations: 14.1 us -> 0.64 us
  local copies, waits for them, and re-layouts: 5.42 us -> 0 us
    pallas_call x0 -> x1, Pallas kernels: none -> 165 us  [shards(): pl.pallas_call(kernel, out_shape=[jax.ShapeDtypeStruct((rows, width), BF1...]
    reduce_scatter x2 -> x0, waiting for transfers between devices: 152 us -> none  [the longest x1 83.1 us: shards(): lax.psum_scatter(times_t(attn, w_out[0]).astype(jnp.bfloat16), 'seq', sca...]
    all_gather x3 -> x0, waiting for transfers between devices: 144 us -> none  [the longest x1 66.6 us: shards(): all_bwd = lax.all_gather(normed_bwd, 'seq', axis=0, tiled=True)]
    dot_general x16 -> x0, matrix products: 78 us -> none  [the longest x1 15.4 us: step(): jnp.einsum('hqk,qhd->khd', score_grad, query_block, preferred_element_typ...]
    sub x2 -> x0, matrix products: 12.5 us -> none  [the longest x1 7.26 us: step(): probs = jax.nn.softmax(scores, axis=-1)]
    ppermute x2 -> x0, waiting for transfers between devices: 9.62 us -> none  [passed_along(): return lax.ppermute(value, axis, pairs)]
    convert_element_type x5 -> x0, other arithmetic: 8.56 us -> none  [the longest x1 2.78 us: normalize(): return ((inputs * inv_rms * gain_row).astype(jnp.bfloat16), inv_rms)]
  transfers between devices with their start and end apart: 7 -> 0, of which waited for: 6 -> 0; matrix products, arithmetic and copies ran while one was open for 21% -> 0% of each run, Pallas kernels for 0% -> 0%
where the time goes in v2:
time: 168 us
  Pallas kernels  165 us (98%)
  other arithmetic  2.76 us (2%)
    pallas_call x1, Pallas kernels, shards(): pl.pallas_call(kernel, out_shape=[jax.ShapeDtypeStruct((rows, width), BF1...  165 us

profile of v2, /device:TPU:0, one launch (start us, length us, event | category | flops | bytes accessed | tf_op | source)
XLA Modules:
  0.0 168.2 jit_solution(16445322311125661551)
XLA Ops:
  0.6 164.8 %relay_attention.1 = (bf16[128,2048]{1,0:T(8,128)(2,1)}, bf16[128,2048]{1,0:T(8,128)(2,1)}) custom-call(f32[128,2048]{1,0:T(8,128)} %bitcast.13, f32[128,2048]{1,0:T(8,128)} %bitcast.14, f32[128,2048]{1,0:T(8,128)} %bitcast.15, f32[1,2048]{1,0:T(1,128)} %gain_ref.1, bf16[2048,256]{1,0:T(8,128)(2,1)} %bitcast.16, bf16[2048,256]{1,0:T(8,128)(2,1)} %bitcast.17, ...), custom_call_target="tpu_custom_call" | custom-call | tf_op jit(solution)/shard_map/relay_attention/pallas_call | solution.py:541
  165.4 2.8 %bitcast_convert_fusion = (f32[1,128,2048]{2,1,0:T(8,128)}, f32[1,128,2048]{2,1,0:T(8,128)}) fusion(bf16[128,2048]{1,0:T(8,128)(2,1)} %get-tuple-element.5, bf16[128,2048]{1,0:T(8,128)(2,1)} %get-tuple-element.4), kind=kLoop, calls=%fused_computation | loop fusion | flops 524288 | bytes 3145728 | tf_op jit(solution)/shard_map/broadcast_in_dim | solution.py:579

commit v3 on v2

v3 whole, which is shorter than its diff:
```python
import math

import jax
import jax.numpy as jnp
import numpy as np
from jax import lax
from jax.experimental import pallas as pl
from jax.experimental.pallas import tpu as pltpu
from jax.sharding import PartitionSpec as P

HD = 128
MESH = pl.DeviceIdType.MESH
F32 = jnp.float32
BF16 = jnp.bfloat16
SCALE = HD ** (-0.5)
LOG2E = math.log2(math.e)


def rope_constants(length):
    inverse = 10000.0 ** (-(np.arange(HD // 2, dtype=np.float64) * 2.0 / HD))
    angles = np.arange(length, dtype=np.float64)[:, None] * inverse[None, :]
    cosine, sine = np.cos(angles), np.sin(angles)
    return (
        np.concatenate([cosine, cosine], 1).astype(np.float32),
        np.concatenate([-sine, sine], 1).astype(np.float32),
    )


def dot_nn(left, right):
    return jnp.dot(left, right, preferred_element_type=F32)


def dot_nt(left, right):
    return lax.dot_general(left, right, (((1,), (1,)), ((), ())), preferred_element_type=F32)


def kernel(
    x_fwd_hbm,
    x_bwd_hbm,
    grad_hbm,
    gain_ref,
    wq_hbm,
    wk_hbm,
    wv_hbm,
    wo_hbm,
    cos_hbm,
    sin_hbm,
    act_ref,
    dgrad_ref,
    x_fwd,
    x_bwd,
    grad,
    wq,
    wk,
    wv,
    wo,
    wo_y,
    cos,
    sin,
    w3t,
    wot,
    gat_f,
    gat_b,
    gat_g,
    q_ref,
    k_ref,
    v_ref,
    g_ref,
    kt_ref,
    vt_ref,
    dk_acc,
    dv_acc,
    dqkv,
    attn,
    attn_y,
    d_send,
    part_b,
    part_f,
    recv_b,
    recv_f,
    out_b,
    out_f,
    load_sem,
    send_sem,
    recv_sem,
):
    rows = x_fwd.shape[0]
    half, quarter = rows // 2, rows // 4
    length, width = gat_f.shape
    feats = wq.shape[1]
    heads = feats // HD
    pipe, seq = lax.axis_index("pipe"), lax.axis_index("seq")
    n_pipe = lax.axis_size("pipe")
    n_x = lax.axis_size("seq") // 2
    my_x, my_y = lax.div(seq, 2), lax.rem(seq, 2)
    left_x, right_x, far_x = (lax.rem(my_x + step, n_x) for step in (n_x - 1, 1, 2))
    own_row, other_row = my_y, 1 - my_y

    def slot(x, y):
        return x * 2 + y

    def at(x, y, start, count):
        return pl.ds(pl.multiple_of(slot(x, y) * rows + start, 16), count)

    others = {"f": far_x, "r": right_x, "l": left_x, "m": my_x}
    devices = {
        "L": (pipe, slot(left_x, my_y)),
        "R": (pipe, slot(right_x, my_y)),
        "Y": (pipe, slot(my_x, 1 - my_y)),
        "N": (lax.rem(pipe + 1, n_pipe), seq),
        "P": (lax.rem(pipe + n_pipe - 1, n_pipe), seq),
    }

    loads = {}

    def load(index, src, dst):
        loads[index] = pltpu.make_async_copy(src, dst, load_sem.at[index])
        loads[index].start()

    load(0, x_bwd_hbm, x_bwd)
    load(1, grad_hbm, grad)
    load(2, x_fwd_hbm, x_fwd)
    load(3, wq_hbm, wq)
    load(4, wk_hbm, wk)
    load(5, wv_hbm, wv)
    load(6, wo_hbm, wo)
    load(7, cos_hbm, cos)
    load(8, sin_hbm, sin)

    barrier = pltpu.get_barrier_semaphore()
    for device in devices.values():
        pl.semaphore_signal(barrier, inc=1, device_id=device, device_id_type=MESH)

    copies = {}

    def describe(name):
        index, refs, where = copies[name]
        src, dst = refs()
        return pltpu.make_async_remote_copy(
            src_ref=src,
            dst_ref=dst,
            send_sem=send_sem.at[index],
            recv_sem=recv_sem.at[index],
            device_id=devices[where],
            device_id_type=MESH,
        )

    def send(name, refs, where):
        copies[name] = (len(copies), refs, where)
        describe(name).start()

    def arrived(name):
        describe(name).wait_recv()

    def normalize_into(source, target):
        def body(i, carry):
            here = pl.ds(pl.multiple_of(i * quarter, quarter), quarter)
            values = source[here, :]
            inv_rms = lax.rsqrt(jnp.mean(values * values, -1, keepdims=True) + 1e-05)
            there = at(my_x, my_y, i * quarter, quarter)
            target[there, :] = (values * inv_rms * gain_ref[...]).astype(BF16)
            return carry

        lax.fori_loop(0, rows // quarter, body, 0)

    def round_into(source, target):
        def body(i, carry):
            here = pl.ds(pl.multiple_of(i * quarter, quarter), quarter)
            target[in_row(my_x, i * quarter, quarter), :] = source[here, :].astype(BF16)
            return carry

        lax.fori_loop(0, rows // quarter, body, 0)

    def pass_on(tag, buf, x, y, start, count, where):
        send(tag + where, lambda: (buf.at[at(x, y, start, count)],) * 2, where)

    def gather_start(tag, buf, split):
        pass_on(tag + "a0", buf, my_x, my_y, 0, split, "Y")
        for where in "LR":
            pass_on(tag + "a0", buf, my_x, my_y, 0, split, where)
        for where in "LRY":
            pass_on(tag + "b0", buf, my_x, my_y, split, rows - split, where)

    def gather_near_a(tag, buf, split):
        part = split // 2
        arrived(tag + "a0R")
        pass_on(tag + "a1", buf, left_x, my_y, 0, part, "R")
        arrived(tag + "a0L")
        pass_on(tag + "a1", buf, right_x, my_y, part, part, "L")

    def gather_cross_a(tag, buf, split):
        arrived(tag + "a0Y")
        for where in "LR":
            pass_on(tag + "a2", buf, my_x, other_row, 0, split, where)

    def gather_near_b(tag, buf, split):
        count = rows - split
        part = count // 2
        arrived(tag + "b0R")
        pass_on(tag + "b1", buf, left_x, my_y, split, part, "R")
        pass_on(tag + "b1l", buf, left_x, my_y, split, count, "Y")
        arrived(tag + "b0L")
        pass_on(tag + "b1", buf, right_x, my_y, split + part, part, "L")
        pass_on(tag + "b1r", buf, right_x, my_y, split, count, "Y")

    def gather_far_b(tag, buf, split):
        part = (rows - split) // 2
        arrived(tag + "b1R")
        pass_on(tag + "b2r", buf, far_x, my_y, split, part, "Y")
        arrived(tag + "b1L")
        pass_on(tag + "b2l", buf, far_x, my_y, split + part, part, "Y")

    def gather_far_a(tag, buf, split):
        part = split // 2
        arrived(tag + "a2R")
        pass_on(tag + "a3", buf, left_x, other_row, 0, part, "R")
        arrived(tag + "a2L")
        pass_on(tag + "a3", buf, right_x, other_row, part, part, "L")

    def gather_end(tag):
        for name in ("a1R", "a1L", "b0Y", "b1lY", "b1rY", "a3R", "a3L", "b2rY", "b2lY"):
            arrived(tag + name)

    def in_row(x, start, count):
        return pl.ds(pl.multiple_of(x * rows + start, 16), count)

    def pass_row(name, x, start, count, where):
        send(name, lambda: (gat_g.at[in_row(x, start, count)],) * 2, where)

    def grad_start():
        pass_row("g0R0", my_x, 0, half, "R")
        pass_row("g0L1", my_x, half, half, "L")
        pass_row("g0R1", my_x, half, half, "R")
        pass_row("g0L0", my_x, 0, half, "L")

    def grad_near():
        arrived("g0R0")
        pass_row("g1R", left_x, 0, half, "R")
        arrived("g0L1")
        pass_row("g1L", right_x, half, half, "L")

    def grad_end():
        for name in ("g0R1", "g0L0", "g1R", "g1L"):
            arrived(name)

    wo_pieces = 8

    def swap_wo(pieces):
        for piece in pieces:
            here = pl.ds(piece * (width // wo_pieces), width // wo_pieces)
            send(f"wo{piece}", lambda here=here: (wo_hbm.at[here], wo_y.at[here]), "Y")

    def wo_arrived():
        for piece in range(wo_pieces):
            arrived(f"wo{piece}")

    def swap_d_attn(x, name):
        send(
            "da" + name,
            lambda: (d_send.at[in_row(x, 0, rows)], g_ref.at[at(x, my_y, 0, rows)]),
            "Y",
        )

    def swap_attn(x, name):
        send(
            "at" + name,
            lambda: (attn.at[at(x, other_row, 0, rows)], attn_y.at[in_row(x, 0, rows)]),
            "Y",
        )

    places = {}
    cursor = 0
    for name, count in (
        ("a0R0", quarter),
        ("a0L0", quarter),
        ("a0R1", quarter),
        ("a0L1", quarter),
        ("a1R0", half),
        ("a1L0", half),
        ("a1R1", half),
        ("a1L1", half),
        ("a2Y", half),
        ("b0Yf", half),
        ("b0Yr", half),
        ("b0Yl", half),
        ("b0Ym", half),
        ("b1R", quarter),
        ("b1L", quarter),
        ("b2R", half),
        ("b2L", half),
    ):
        places[name] = (cursor, count)
        cursor += count
    places.update({"f0R": (0, half), "f0L": (half, half), "f1R": (rows, rows), "f1L": (2 * rows, rows)})

    def to(name, place, offset, part, recv, here, count, where):
        start = places[place][0] + offset
        send(name, lambda: (part.at[here()], recv.at[pl.ds(start, count)]), where)

    def add_in(part, recv, place, here):
        start, count = places[place]
        part[here, :] = (
            part[here, :].astype(F32) + recv[pl.ds(start, count), :].astype(F32)
        ).astype(BF16)

    def to_b(place, x, y, start, count, where, suffix="", offset=0):
        to(
            "RB" + place + suffix,
            place,
            offset,
            part_b,
            recv_b,
            lambda: at(x, y, start, count),
            count,
            where,
        )

    def reduce_far():
        for w, y in ((1, other_row), (0, own_row)):
            to_b(f"a0R{w}", far_x, y, 0, quarter, "R")
            to_b(f"a0L{w}", far_x, y, quarter, quarter, "L")
        to_b("b0Yf", far_x, other_row, half, half, "Y")

    def reduce_right():
        to_b("b0Yr", right_x, other_row, half, half, "Y")
        for w, y in ((1, other_row), (0, own_row)):
            to_b(f"a1R{w}", right_x, y, quarter, quarter, "R", "i", quarter)

    def reduce_left():
        to_b("b0Yl", left_x, other_row, half, half, "Y")
        for w, y in ((1, other_row), (0, own_row)):
            to_b(f"a1L{w}", left_x, y, 0, quarter, "L", "i", 0)

    def reduce_mine():
        to_b("b0Ym", my_x, other_row, half, half, "Y")

    def reduce_near_a():
        for w, y in ((1, other_row), (0, own_row)):
            arrived(f"RBa0R{w}")
            add_in(part_b, recv_b, f"a0R{w}", at(right_x, y, 0, quarter))
            to_b(f"a1R{w}", right_x, y, 0, quarter, "R", "d", 0)
            arrived(f"RBa0L{w}")
            add_in(part_b, recv_b, f"a0L{w}", at(left_x, y, quarter, quarter))
            to_b(f"a1L{w}", left_x, y, quarter, quarter, "L", "d", quarter)

    def reduce_far_b():
        arrived("RBb0Yf")
        add_in(part_b, recv_b, "b0Yf", at(far_x, own_row, half, half))
        to_b("b1R", far_x, own_row, half, quarter, "R")
        to_b("b1L", far_x, own_row, half + quarter, quarter, "L")
        arrived("RBb0Yr")
        add_in(part_b, recv_b, "b0Yr", at(right_x, own_row, half, half))
        to_b("b2R", right_x, own_row, half + quarter, quarter, "R", "i", quarter)
        arrived("RBb0Yl")
        add_in(part_b, recv_b, "b0Yl", at(left_x, own_row, half, half))
        to_b("b2L", left_x, own_row, half, quarter, "L", "i", 0)

    def arrived_both(name):
        arrived(name + "i")
        arrived(name + "d")

    def reduce_cross_a():
        for place in ("a1R1", "a1L1"):
            arrived_both("RB" + place)
            add_in(part_b, recv_b, place, at(my_x, other_row, 0, half))
        to_b("a2Y", my_x, other_row, 0, half, "Y")

    def reduce_near_b():
        arrived("RBb1R")
        add_in(part_b, recv_b, "b1R", at(right_x, own_row, half, quarter))
        to_b("b2R", right_x, own_row, half, quarter, "R", "d", 0)
        arrived("RBb1L")
        add_in(part_b, recv_b, "b1L", at(left_x, own_row, half + quarter, quarter))
        to_b("b2L", left_x, own_row, half + quarter, quarter, "L", "d", quarter)

    def last_a():
        arrived_both("RBa1R0")
        arrived_both("RBa1L0")
        arrived("RBa2Y")
        return ("a1R0", "a1L0", "a2Y")

    def last_b():
        arrived_both("RBb2R")
        arrived_both("RBb2L")
        arrived("RBb0Ym")
        return ("b2R", "b2L", "b0Ym")

    def to_f(place, x, start, where, suffix="", offset=0):
        to(
            "RF" + place + suffix,
            place,
            offset,
            part_f,
            recv_f,
            lambda: in_row(x, start, half),
            half,
            where,
        )

    def row_far():
        to_f("f0R", far_x, 0, "R")
        to_f("f0L", far_x, half, "L")

    def row_right():
        to_f("f1R", right_x, half, "R", "i", half)

    def row_left():
        to_f("f1L", left_x, 0, "L", "i", 0)

    def row_near():
        arrived("RFf0R")
        add_in(part_f, recv_f, "f0R", in_row(right_x, 0, half))
        to_f("f1R", right_x, 0, "R", "d", 0)
        arrived("RFf0L")
        add_in(part_f, recv_f, "f0L", in_row(left_x, half, half))
        to_f("f1L", left_x, half, "L", "d", half)

    step_rows = 16

    def total_of(part, base, recv, spans, offset):
        total = part[pl.ds(pl.multiple_of(base + offset, step_rows), step_rows), :].astype(F32)
        for start in spans:
            total += recv[pl.ds(start + offset, step_rows), :].astype(F32)
        return total

    def finish_act(start, name):
        spans = [places[place][0] + start for place in ("f1R", "f1L")]

        def body(i, carry):
            offset = pl.multiple_of(i * step_rows, step_rows)
            here = pl.ds(start + offset, step_rows)
            total = total_of(part_f, my_x * rows + start, recv_f, spans, offset)
            out_f[here, :] = (x_fwd[here, :] + total).astype(BF16)
            return carry

        lax.fori_loop(0, half // step_rows, body, 0)
        send(name, lambda: (out_f.at[pl.ds(start, half)], act_ref.at[pl.ds(start, half)]), "N")

    def finish_grad(names, start, name):
        spans = [places[place][0] for place in names]

        def body(i, carry):
            offset = pl.multiple_of(i * step_rows, step_rows)
            here = pl.ds(start + offset, step_rows)
            saved = x_bwd[here, :]
            inv_rms = lax.rsqrt(jnp.mean(saved * saved, -1, keepdims=True) + 1e-05)
            total = total_of(part_b, slot(my_x, my_y) * rows + start, recv_b, spans, offset)
            gain_grad = total * gain_ref[...]
            mean = jnp.mean(saved * gain_grad, -1, keepdims=True)
            d_input = inv_rms * gain_grad - saved * (inv_rms * inv_rms * inv_rms * mean)
            out_b[here, :] = (grad[here, :] + d_input).astype(BF16)
            return carry

        lax.fori_loop(0, half // step_rows, body, 0)
        send(name, lambda: (out_b.at[pl.ds(start, half)], dgrad_ref.at[pl.ds(start, half)]), "P")

    block = 256
    blocks = length // block

    def rotated(values, here, sign):
        out = values * cos[here, :]
        turned = pltpu.roll(values, HD // 2, 1) * sin[here, :]
        return out + turned if sign > 0 else out - turned

    def project(buf):
        def body(i, carry):
            here = pl.ds(pl.multiple_of(i * block, block), block)
            normed = buf[here, :]
            query = dot_nn(normed, wq[...])
            key = dot_nn(normed, wk[...])
            for h in range(heads):
                head = slice(h * HD, (h + 1) * HD)
                q_ref[here, head] = rotated(query[:, head], here, 1).astype(BF16)
                turned = rotated(key[:, head], here, 1)
                k_ref[here, head] = turned.astype(BF16)
                kt_ref[head, here] = turned.T.astype(BF16)
            value = dot_nn(normed, wv[...])
            v_ref[here, :] = value.astype(BF16)
            vt_ref[:, here] = value.T.astype(BF16)
            return carry

        lax.fori_loop(0, blocks, body, 0)

    def project_grad():
        def cross(x, carry):
            here = in_row(x, 0, rows)
            d_send[here, :] = dot_nn(gat_g[here, :], wo_y[...]).astype(BF16)
            return carry

        lax.fori_loop(0, n_x, cross, 0)
        for name, x in others.items():
            swap_d_attn(x, name)

        def own(x, carry):
            there = at(x, my_y, 0, rows)
            g_ref[there, :] = dot_nn(gat_g[in_row(x, 0, rows), :], wo[...]).astype(BF16)
            return carry

        lax.fori_loop(0, n_x, own, 0)

    def run_actions(actions, h, i):
        for number, todo in actions.items():
            if number // blocks == h:

                @pl.when(i == number % blocks)
                def _(todo=todo):
                    for act in todo:
                        act()

    def exponentials(h, here):
        head = slice(h * HD, (h + 1) * HD)
        scores = dot_nt(k_ref[:, head], q_ref[here, head])
        top = jnp.max(scores, axis=0, keepdims=True)
        weights = jnp.exp2((scores - top) * (SCALE * LOG2E))
        return weights, 1.0 / jnp.sum(weights, axis=0, keepdims=True)

    def attend_back(actions):
        for h in range(heads):
            head = slice(h * HD, (h + 1) * HD)
            dk_acc[...] = jnp.zeros_like(dk_acc)
            dv_acc[...] = jnp.zeros_like(dv_acc)

            def body(i, carry, h=h, head=head):
                run_actions(actions, h, i)
                here = pl.ds(pl.multiple_of(i * block, block), block)
                weights, inverse = exponentials(h, here)
                probs = weights * inverse
                d_out = g_ref[here, head]
                dv_acc[...] += dot_nn(probs.astype(BF16), d_out)
                d_probs = dot_nt(v_ref[:, head], d_out)
                delta = jnp.sum(probs * d_probs, axis=0, keepdims=True)
                d_scores = (probs * (d_probs - delta) * SCALE).astype(BF16)
                dk_acc[...] += dot_nn(d_scores, q_ref[here, head])
                d_query = dot_nn(kt_ref[head, :], d_scores).T
                dqkv[here, head] = rotated(d_query, here, -1).astype(BF16)
                return carry

            lax.fori_loop(0, blocks, body, 0)

            def close(i, carry, h=h):
                here = pl.ds(pl.multiple_of(i * block, block), block)
                d_key = rotated(dk_acc[here, :], here, -1)
                dqkv[here, feats + h * HD : feats + (h + 1) * HD] = d_key.astype(BF16)
                dqkv[here, 2 * feats + h * HD : 2 * feats + (h + 1) * HD] = dv_acc[here, :].astype(BF16)
                return carry

            lax.fori_loop(0, blocks, close, 0)

    def attend(x):
        def body(i, carry):
            here = pl.ds(pl.multiple_of(x * block, block), block)
            for h in range(heads):
                head = slice(h * HD, (h + 1) * HD)
                weights, inverse = exponentials(h, here)
                out = dot_nn(vt_ref[head, :], weights.astype(BF16)) * inverse
                attn[here, head] = out.T.astype(BF16)
            return carry

        lax.fori_loop(0, 1, body, 0)

    columns = 512

    def multiply_out_b(x):
        here = pl.ds(pl.multiple_of(x * block, block), block)

        def body(i, carry):
            there = pl.ds(pl.multiple_of(i * columns, columns), columns)
            part_b[here, there] = dot_nn(dqkv[here, :], w3t[:, there]).astype(BF16)
            return carry

        lax.fori_loop(0, width // columns, body, 0)

    def multiply_out_f(x):
        here = in_row(x, 0, rows)
        both = jnp.concatenate([attn[at(x, my_y, 0, rows), :], attn_y[here, :]], 1)

        def body(i, carry):
            there = pl.ds(pl.multiple_of(i * columns, columns), columns)
            part_f[here, there] = dot_nn(both, wot[:, there]).astype(BF16)
            return carry

        lax.fori_loop(0, width // columns, body, 0)

    def transpose_into(source, target, offset):
        def body(i, carry):
            here = pl.ds(pl.multiple_of(i * feats, feats), feats)
            target[offset : offset + feats, here] = source[here, :].T
            return carry

        lax.fori_loop(0, width // feats, body, 0)

    split_b, split_f = half + quarter, half
    loads[0].wait()
    normalize_into(x_bwd, gat_b)
    pl.semaphore_wait(barrier, len(devices))
    gather_start("B", gat_b, split_b)
    swap_wo(range(0, 4))
    loads[1].wait()
    round_into(grad, gat_g)
    loads[2].wait()
    normalize_into(x_fwd, gat_f)
    gather_near_a("B", gat_b, split_b)
    gather_cross_a("B", gat_b, split_b)
    grad_start()
    for index in range(3, 9):
        loads[index].wait()
    transpose_into(wq, w3t, 0)
    gather_near_b("B", gat_b, split_b)
    swap_wo(range(4, 8))
    gather_far_b("B", gat_b, split_b)
    transpose_into(wk, w3t, feats)
    gather_far_a("B", gat_b, split_b)
    grad_near()
    gather_start("F", gat_f, split_f)
    transpose_into(wv, w3t, 2 * feats)
    transpose_into(wo, wot, 0)
    gather_end("B")
    project(gat_b)
    gather_near_a("F", gat_f, split_f)
    gather_cross_a("F", gat_f, split_f)
    wo_arrived()
    grad_end()
    project_grad()
    transpose_into(wo_y, wot, feats)
    gather_near_b("F", gat_f, split_f)
    for name in others:
        arrived("da" + name)
    attend_back(
        {
            2: [lambda: gather_far_b("F", gat_f, split_f)],
            3: [lambda: gather_far_a("F", gat_f, split_f)],
        }
    )

    multiply_out_b(far_x)
    reduce_far()
    multiply_out_b(right_x)
    reduce_right()
    multiply_out_b(left_x)
    reduce_left()
    multiply_out_b(my_x)
    reduce_mine()
    gather_end("F")
    project(gat_f)
    reduce_near_a()
    attend(far_x)
    swap_attn(far_x, "f")
    reduce_far_b()
    attend(right_x)
    swap_attn(right_x, "r")
    attend(left_x)
    swap_attn(left_x, "l")
    reduce_cross_a()
    arrived("atf")
    multiply_out_f(far_x)
    row_far()
    reduce_near_b()
    arrived("atr")
    multiply_out_f(right_x)
    row_right()
    arrived("atl")
    multiply_out_f(left_x)
    row_left()
    attend(my_x)
    swap_attn(my_x, "m")
    row_near()
    finish_grad(last_a(), 0, "PBa")
    finish_grad(last_b(), half, "PBb")
    arrived("atm")
    multiply_out_f(my_x)
    arrived("RFf1Rd")
    arrived("RFf1Li")
    finish_act(0, "PFa")
    arrived("RFf1Ri")
    arrived("RFf1Ld")
    finish_act(half, "PFb")
    for name in ("PBa", "PBb", "PFa", "PFb"):
        arrived(name)
    for name in copies:
        describe(name).wait_send()


def shards(x_fwd, x_bwd, grad_in, gain, w_query, w_key, w_value, w_out):
    rows, width = x_fwd.shape[1:]
    feats = w_query.shape[2]
    length = rows * lax.axis_size("seq")
    cosine, sine = (jnp.asarray(table) for table in rope_constants(length))
    anywhere = pl.BlockSpec(memory_space=pl.ANY)
    vmem = pltpu.VMEM
    n_copies = 104
    act, dgrad = pl.pallas_call(
        kernel,
        out_shape=[jax.ShapeDtypeStruct((rows, width), BF16)] * 2,
        in_specs=[anywhere] * 3 + [pl.BlockSpec(memory_space=pltpu.VMEM)] + [anywhere] * 6,
        out_specs=[anywhere] * 2,
        scratch_shapes=[vmem((rows, width), F32)] * 3
        + [vmem((width, feats), BF16)] * 5
        + [vmem((length, HD), F32)] * 2
        + [vmem((3 * feats, width), BF16), vmem((2 * feats, width), BF16)]
        + [vmem((length, width), BF16)] * 2
        + [vmem((length // 2, width), BF16)]
        + [vmem((length, feats), BF16)] * 4
        + [vmem((feats, length), BF16)] * 2
        + [vmem((length, HD), F32)] * 2
        + [vmem((length, 3 * feats), BF16), vmem((length, feats), BF16)]
        + [vmem((length // 2, feats), BF16)] * 2
        + [vmem((length, width), BF16), vmem((length // 2, width), BF16)]
        + [vmem((rows * 7, width), BF16), vmem((rows * 3, width), BF16)]
        + [vmem((rows, width), BF16)] * 2
        + [
            pltpu.SemaphoreType.DMA((9,)),
            pltpu.SemaphoreType.DMA((n_copies,)),
            pltpu.SemaphoreType.DMA((n_copies,)),
        ],
        compiler_params=pltpu.CompilerParams(
            collective_id=0, has_side_effects=True, vmem_limit_bytes=67_043_328
        ),
        name="relay_attention",
    )(
        x_fwd[0],
        x_bwd[0],
        grad_in[0],
        gain,
        w_query[0],
        w_key[0],
        w_value[0],
        w_out[0],
        cosine,
        sine,
    )
    return (act.astype(F32)[None], dgrad.astype(F32)[None])


def solution(mesh):
    placed = (
        P("pipe", "seq", None),
        P("pipe", "seq", None),
        P("pipe", "seq", None),
        P("pipe", None),
        P("pipe", None, "seq"),
        P("pipe", None, "seq"),
        P("pipe", None, "seq"),
        P("pipe", None, "seq"),
    )
    return jax.shard_map(
        shards,
        mesh=mesh,
        in_specs=placed,
        out_specs=(P("pipe", "seq", None), P("pipe", "seq", None)),
        check_vma=False,
    )
```

time: 168 us -> 148 us (0.88)
  Pallas kernels: 165 us -> 145 us
    pallas_call x1, Pallas kernels: 165 us -> 145 us  [shards(): pl.pallas_call(kernel, out_shape=[jax.ShapeDtypeStruct((rows, width), BF1...]
where the time goes in v3:
time: 148 us
  Pallas kernels  145 us (98%)
  other arithmetic  2.76 us (2%)
    pallas_call x1, Pallas kernels, shards(): pl.pallas_call(kernel, out_shape=[jax.ShapeDtypeStruct((rows, width), BF1...  145 us

profile of v3, /device:TPU:0, one launch (start us, length us, event | category | flops | bytes accessed | tf_op | source)
XLA Modules:
  0.0 148.0 jit_solution(9221462462232414016)
XLA Ops:
  0.6 144.5 %relay_attention.1 = (bf16[128,2048]{1,0:T(8,128)(2,1)}, bf16[128,2048]{1,0:T(8,128)(2,1)}) custom-call(f32[128,2048]{1,0:T(8,128)} %bitcast.13, f32[128,2048]{1,0:T(8,128)} %bitcast.14, f32[128,2048]{1,0:T(8,128)} %bitcast.15, f32[1,2048]{1,0:T(1,128)} %gain_ref.1, bf16[2048,256]{1,0:T(8,128)(2,1)} %bitcast.16, bf16[2048,256]{1,0:T(8,128)(2,1)} %bitcast.17, ...), custom_call_target="tpu_custom_call" | custom-call | tf_op jit(solution)/shard_map/relay_attention/pallas_call | solution.py:691
  145.2 2.8 %bitcast_convert_fusion = (f32[1,128,2048]{2,1,0:T(8,128)}, f32[1,128,2048]{2,1,0:T(8,128)}) fusion(bf16[128,2048]{1,0:T(8,128)(2,1)} %get-tuple-element.5, bf16[128,2048]{1,0:T(8,128)(2,1)} %get-tuple-element.4), kind=kLoop, calls=%fused_computation | loop fusion | flops 524288 | bytes 3145728 | tf_op jit(solution)/shard_map/broadcast_in_dim | solution.py:731

commit v4 on v3

--- a/solution.py
+++ b/solution.py
@@ -119,13 +119,6 @@
 
     load(0, x_bwd_hbm, x_bwd)
     load(1, grad_hbm, grad)
-    load(2, x_fwd_hbm, x_fwd)
-    load(3, wq_hbm, wq)
-    load(4, wk_hbm, wk)
-    load(5, wv_hbm, wv)
-    load(6, wo_hbm, wo)
-    load(7, cos_hbm, cos)
-    load(8, sin_hbm, sin)
 
     barrier = pltpu.get_barrier_semaphore()
     for device in devices.values():
@@ -174,10 +167,12 @@
     def pass_on(tag, buf, x, y, start, count, where):
         send(tag + where, lambda: (buf.at[at(x, y, start, count)],) * 2, where)
 
-    def gather_start(tag, buf, split):
+    def gather_start_a(tag, buf, split):
         pass_on(tag + "a0", buf, my_x, my_y, 0, split, "Y")
         for where in "LR":
             pass_on(tag + "a0", buf, my_x, my_y, 0, split, where)
+
+    def gather_start_b(tag, buf, split):
         for where in "LRY":
             pass_on(tag + "b0", buf, my_x, my_y, split, rows - split, where)
 
@@ -194,14 +189,15 @@
             pass_on(tag + "a2", buf, my_x, other_row, 0, split, where)
 
     def gather_near_b(tag, buf, split):
-        count = rows - split
-        part = count // 2
+        part = (rows - split) // 2
         arrived(tag + "b0R")
         pass_on(tag + "b1", buf, left_x, my_y, split, part, "R")
-        pass_on(tag + "b1l", buf, left_x, my_y, split, count, "Y")
         arrived(tag + "b0L")
         pass_on(tag + "b1", buf, right_x, my_y, split + part, part, "L")
-        pass_on(tag + "b1r", buf, right_x, my_y, split, count, "Y")
+
+    def gather_near_by(tag, buf, split):
+        pass_on(tag + "b1l", buf, left_x, my_y, split, rows - split, "Y")
+        pass_on(tag + "b1r", buf, right_x, my_y, split, rows - split, "Y")
 
     def gather_far_b(tag, buf, split):
         part = (rows - split) // 2
@@ -268,30 +264,37 @@
             "Y",
         )
 
+    split_r = 64
+    rest = rows - split_r
+    part_a, part_c = split_r // 2, rest // 2
+    groups = ((0, 64), (64, 32), (96, 32))
     places = {}
     cursor = 0
     for name, count in (
-        ("a0R0", quarter),
-        ("a0L0", quarter),
-        ("a0R1", quarter),
-        ("a0L1", quarter),
-        ("a1R0", half),
-        ("a1L0", half),
-        ("a1R1", half),
-        ("a1L1", half),
-        ("a2Y", half),
-        ("b0Yf", half),
-        ("b0Yr", half),
-        ("b0Yl", half),
-        ("b0Ym", half),
-        ("b1R", quarter),
-        ("b1L", quarter),
-        ("b2R", half),
-        ("b2L", half),
+        ("a0R0", part_a),
+        ("a0L0", part_a),
+        ("a0R1", part_a),
+        ("a0L1", part_a),
+        ("a1R0", split_r),
+        ("a1L0", split_r),
+        ("a1R1", split_r),
+        ("a1L1", split_r),
+        ("a2Y", split_r),
+        ("b0Yf", rest),
+        ("b0Yr", rest),
+        ("b0Yl", rest),
+        ("b0Ym", rest),
+        ("b1R", part_c),
+        ("b1L", part_c),
+        ("b2R", rest),
+        ("b2L", rest),
     ):
         places[name] = (cursor, count)
         cursor += count
-    places.update({"f0R": (0, half), "f0L": (half, half), "f1R": (rows, rows), "f1L": (2 * rows, rows)})
+    for number, (start, count) in enumerate(groups):
+        places[f"f0R{number}"] = (start // 2, count // 2)
+        places[f"f0L{number}"] = (half + start // 2, count // 2)
+    places.update({"f1R": (rows, rows), "f1L": (2 * rows, rows)})
 
     def to(name, place, offset, part, recv, here, count, where):
         start = places[place][0] + offset
@@ -317,43 +320,42 @@
 
     def reduce_far():
         for w, y in ((1, other_row), (0, own_row)):
-            to_b(f"a0R{w}", far_x, y, 0, quarter, "R")
-            to_b(f"a0L{w}", far_x, y, quarter, quarter, "L")
-        to_b("b0Yf", far_x, other_row, half, half, "Y")
+            to_b(f"a0R{w}", far_x, y, 0, part_a, "R")
+            to_b(f"a0L{w}", far_x, y, part_a, part_a, "L")
+
+    def reduce_cross(name, x):
+        to_b("b0Y" + name, x, other_row, split_r, rest, "Y")
 
     def reduce_right():
-        to_b("b0Yr", right_x, other_row, half, half, "Y")
         for w, y in ((1, other_row), (0, own_row)):
-            to_b(f"a1R{w}", right_x, y, quarter, quarter, "R", "i", quarter)
+            to_b(f"a1R{w}", right_x, y, part_a, part_a, "R", "i", part_a)
 
     def reduce_left():
-        to_b("b0Yl", left_x, other_row, half, half, "Y")
         for w, y in ((1, other_row), (0, own_row)):
-            to_b(f"a1L{w}", left_x, y, 0, quarter, "L", "i", 0)
-
-    def reduce_mine():
-        to_b("b0Ym", my_x, other_row, half, half, "Y")
-
-    def reduce_near_a():
-        for w, y in ((1, other_row), (0, own_row)):
-            arrived(f"RBa0R{w}")
-            add_in(part_b, recv_b, f"a0R{w}", at(right_x, y, 0, quarter))
-            to_b(f"a1R{w}", right_x, y, 0, quarter, "R", "d", 0)
-            arrived(f"RBa0L{w}")
-            add_in(part_b, recv_b, f"a0L{w}", at(left_x, y, quarter, quarter))
-            to_b(f"a1L{w}", left_x, y, quarter, quarter, "L", "d", quarter)
+            to_b(f"a1L{w}", left_x, y, 0, part_a, "L", "i", 0)
+
+    def reduce_near_a(w):
+        y = (own_row, other_row)[w]
+        arrived(f"RBa0R{w}")
+        add_in(part_b, recv_b, f"a0R{w}", at(right_x, y, 0, part_a))
+        to_b(f"a1R{w}", right_x, y, 0, part_a, "R", "d", 0)
+        arrived(f"RBa0L{w}")
+        add_in(part_b, recv_b, f"a0L{w}", at(left_x, y, part_a, part_a))
+        to_b(f"a1L{w}", left_x, y, part_a, part_a, "L", "d", part_a)
 
     def reduce_far_b():
         arrived("RBb0Yf")
-        add_in(part_b, recv_b, "b0Yf", at(far_x, own_row, half, half))
-        to_b("b1R", far_x, own_row, half, quarter, "R")
-        to_b("b1L", far_x, own_row, half + quarter, quarter, "L")
+        add_in(part_b, recv_b, "b0Yf", at(far_x, own_row, split_r, rest))
+        to_b("b1R", far_x, own_row, split_r, part_c, "R")
+        to_b("b1L", far_x, own_row, split_r + part_c, part_c, "L")
+
+    def reduce_side_b():
         arrived("RBb0Yr")
-        add_in(part_b, recv_b, "b0Yr", at(right_x, own_row, half, half))
-        to_b("b2R", right_x, own_row, half + quarter, quarter, "R", "i", quarter)
+        add_in(part_b, recv_b, "b0Yr", at(right_x, own_row, split_r, rest))
+        to_b("b2R", right_x, own_row, split_r + part_c, part_c, "R", "i", part_c)
         arrived("RBb0Yl")
-        add_in(part_b, recv_b, "b0Yl", at(left_x, own_row, half, half))
-        to_b("b2L", left_x, own_row, half, quarter, "L", "i", 0)
+        add_in(part_b, recv_b, "b0Yl", at(left_x, own_row, split_r, rest))
+        to_b("b2L", left_x, own_row, split_r, part_c, "L", "i", 0)
 
     def arrived_both(name):
         arrived(name + "i")
@@ -362,58 +364,50 @@
     def reduce_cross_a():
         for place in ("a1R1", "a1L1"):
             arrived_both("RB" + place)
-            add_in(part_b, recv_b, place, at(my_x, other_row, 0, half))
-        to_b("a2Y", my_x, other_row, 0, half, "Y")
+            add_in(part_b, recv_b, place, at(my_x, other_row, 0, split_r))
+        to_b("a2Y", my_x, other_row, 0, split_r, "Y")
 
     def reduce_near_b():
         arrived("RBb1R")
-        add_in(part_b, recv_b, "b1R", at(right_x, own_row, half, quarter))
-        to_b("b2R", right_x, own_row, half, quarter, "R", "d", 0)
+        add_in(part_b, recv_b, "b1R", at(right_x, own_row, split_r, part_c))
+        to_b("b2R", right_x, own_row, split_r, part_c, "R", "d", 0)
         arrived("RBb1L")
-        add_in(part_b, recv_b, "b1L", at(left_x, own_row, half + quarter, quarter))
-        to_b("b2L", left_x, own_row, half + quarter, quarter, "L", "d", quarter)
-
-    def last_a():
-        arrived_both("RBa1R0")
-        arrived_both("RBa1L0")
-        arrived("RBa2Y")
-        return ("a1R0", "a1L0", "a2Y")
-
-    def last_b():
-        arrived_both("RBb2R")
-        arrived_both("RBb2L")
-        arrived("RBb0Ym")
-        return ("b2R", "b2L", "b0Ym")
-
-    def to_f(place, x, start, where, suffix="", offset=0):
+        add_in(part_b, recv_b, "b1L", at(left_x, own_row, split_r + part_c, part_c))
+        to_b("b2L", left_x, own_row, split_r + part_c, part_c, "L", "d", part_c)
+
+    def to_f(place, x, start, count, where, name, offset=0):
         to(
-            "RF" + place + suffix,
+            "RF" + name,
             place,
             offset,
             part_f,
             recv_f,
-            lambda: in_row(x, start, half),
-            half,
+            lambda: in_row(x, start, count),
+            count,
             where,
         )
 
     def row_far():
-        to_f("f0R", far_x, 0, "R")
-        to_f("f0L", far_x, half, "L")
-
-    def row_right():
-        to_f("f1R", right_x, half, "R", "i", half)
-
-    def row_left():
-        to_f("f1L", left_x, 0, "L", "i", 0)
-
-    def row_near():
-        arrived("RFf0R")
-        add_in(part_f, recv_f, "f0R", in_row(right_x, 0, half))
-        to_f("f1R", right_x, 0, "R", "d", 0)
-        arrived("RFf0L")
-        add_in(part_f, recv_f, "f0L", in_row(left_x, half, half))
-        to_f("f1L", left_x, half, "L", "d", half)
+        for number, (start, count) in enumerate(groups):
+            to_f(f"f0R{number}", far_x, start, count // 2, "R", f"f0R{number}")
+            to_f(f"f0L{number}", far_x, start + count // 2, count // 2, "L", f"f0L{number}")
+
+    def row_right(number):
+        start, part = groups[number][0], groups[number][1] // 2
+        to_f("f1R", right_x, start + part, part, "R", f"f1R{number}i", start + part)
+
+    def row_left(number):
+        start, part = groups[number][0], groups[number][1] // 2
+        to_f("f1L", left_x, start, part, "L", f"f1L{number}i", start)
+
+    def row_near(number):
+        start, part = groups[number][0], groups[number][1] // 2
+        arrived(f"RFf0R{number}")
+        add_in(part_f, recv_f, f"f0R{number}", in_row(right_x, start, part))
+        to_f("f1R", right_x, start, part, "R", f"f1R{number}d", start)
+        arrived(f"RFf0L{number}")
+        add_in(part_f, recv_f, f"f0L{number}", in_row(left_x, start + part, part))
+        to_f("f1L", left_x, start + part, part, "L", f"f1L{number}d", start + part)
 
     step_rows = 16
 
@@ -423,8 +417,11 @@
             total += recv[pl.ds(start + offset, step_rows), :].astype(F32)
         return total
 
-    def finish_act(start, name):
+    def finish_act(number):
+        start, count = groups[number]
         spans = [places[place][0] + start for place in ("f1R", "f1L")]
+        arrived_both(f"RFf1R{number}")
+        arrived_both(f"RFf1L{number}")
 
         def body(i, carry):
             offset = pl.multiple_of(i * step_rows, step_rows)
@@ -433,10 +430,24 @@
             out_f[here, :] = (x_fwd[here, :] + total).astype(BF16)
             return carry
 
-        lax.fori_loop(0, half // step_rows, body, 0)
-        send(name, lambda: (out_f.at[pl.ds(start, half)], act_ref.at[pl.ds(start, half)]), "N")
-
-    def finish_grad(names, start, name):
+        lax.fori_loop(0, count // step_rows, body, 0)
+        send(
+            f"PF{number}",
+            lambda: (out_f.at[pl.ds(start, count)], act_ref.at[pl.ds(start, count)]),
+            "N",
+        )
+
+    def finish_grad(last):
+        if last:
+            start, count, names = split_r, rest, ("b2R", "b2L", "b0Ym")
+            arrived_both("RBb2R")
+            arrived_both("RBb2L")
+            arrived("RBb0Ym")
+        else:
+            start, count, names = 0, split_r, ("a1R0", "a1L0", "a2Y")
+            arrived_both("RBa1R0")
+            arrived_both("RBa1L0")
+            arrived("RBa2Y")
         spans = [places[place][0] for place in names]
 
         def body(i, carry):
@@ -451,8 +462,12 @@
             out_b[here, :] = (grad[here, :] + d_input).astype(BF16)
             return carry
 
-        lax.fori_loop(0, half // step_rows, body, 0)
-        send(name, lambda: (out_b.at[pl.ds(start, half)], dgrad_ref.at[pl.ds(start, half)]), "P")
+        lax.fori_loop(0, count // step_rows, body, 0)
+        send(
+            f"PB{last}",
+            lambda: (out_b.at[pl.ds(start, count)], dgrad_ref.at[pl.ds(start, count)]),
+            "P",
+        )
 
     block = 256
     blocks = length // block
@@ -481,22 +496,27 @@
 
         lax.fori_loop(0, blocks, body, 0)
 
-    def project_grad():
-        def cross(x, carry):
+    def project_grad_cross():
+        def body(x, carry):
             here = in_row(x, 0, rows)
             d_send[here, :] = dot_nn(gat_g[here, :], wo_y[...]).astype(BF16)
             return carry
 
-        lax.fori_loop(0, n_x, cross, 0)
+        lax.fori_loop(0, n_x, body, 0)
         for name, x in others.items():
             swap_d_attn(x, name)
 
-        def own(x, carry):
+    def project_grad_own():
+        def body(x, carry):
             there = at(x, my_y, 0, rows)
             g_ref[there, :] = dot_nn(gat_g[in_row(x, 0, rows), :], wo[...]).astype(BF16)
             return carry
 
-        lax.fori_loop(0, n_x, own, 0)
+        lax.fori_loop(0, n_x, body, 0)
+
+    def d_attn_arrived():
+        for name in others:
+            arrived("da" + name)
 
     def run_actions(actions, h, i):
         for number, todo in actions.items():
@@ -589,92 +609,124 @@
 
         lax.fori_loop(0, width // feats, body, 0)
 
-    split_b, split_f = half + quarter, half
+    split_b, split_f = 96, 64
+    pl.semaphore_wait(barrier, len(devices))
+    swap_wo(range(0, 1))
     loads[0].wait()
+    load(2, x_fwd_hbm, x_fwd)
+    load(3, wo_hbm, wo)
+    load(4, wq_hbm, wq)
+    load(5, wk_hbm, wk)
+    load(6, wv_hbm, wv)
+    load(7, cos_hbm, cos)
+    load(8, sin_hbm, sin)
     normalize_into(x_bwd, gat_b)
-    pl.semaphore_wait(barrier, len(devices))
-    gather_start("B", gat_b, split_b)
-    swap_wo(range(0, 4))
+    gather_start_b("B", gat_b, split_b)
     loads[1].wait()
     round_into(grad, gat_g)
+    gather_start_a("B", gat_b, split_b)
     loads[2].wait()
     normalize_into(x_fwd, gat_f)
-    gather_near_a("B", gat_b, split_b)
-    gather_cross_a("B", gat_b, split_b)
-    grad_start()
     for index in range(3, 9):
         loads[index].wait()
-    transpose_into(wq, w3t, 0)
     gather_near_b("B", gat_b, split_b)
-    swap_wo(range(4, 8))
+    swap_wo(range(6, 7))
+    gather_near_by("B", gat_b, split_b)
+    grad_start()
+    swap_wo(range(5, 6))
+    transpose_into(wk, w3t, feats)
+    swap_wo(range(7, 8))
+    swap_wo(range(1, 2))
+    swap_wo(range(3, 4))
+    gather_cross_a("B", gat_b, split_b)
     gather_far_b("B", gat_b, split_b)
-    transpose_into(wk, w3t, feats)
+    grad_near()
+    swap_wo(range(4, 5))
+    swap_wo(range(2, 3))
     gather_far_a("B", gat_b, split_b)
-    grad_near()
-    gather_start("F", gat_f, split_f)
-    transpose_into(wv, w3t, 2 * feats)
+    gather_near_a("B", gat_b, split_b)
+    gather_start_b("F", gat_f, split_f)
+    grad_end()
+    project_grad_own()
+    wo_arrived()
+    project_grad_cross()
+    gather_start_a("F", gat_f, split_f)
+    transpose_into(wo_y, wot, feats)
     transpose_into(wo, wot, 0)
     gather_end("B")
     project(gat_b)
-    gather_near_a("F", gat_f, split_f)
-    gather_cross_a("F", gat_f, split_f)
-    wo_arrived()
-    grad_end()
-    project_grad()
-    transpose_into(wo_y, wot, feats)
+    transpose_into(wq, w3t, 0)
     gather_near_b("F", gat_f, split_f)
-    for name in others:
-        arrived("da" + name)
+    d_attn_arrived()
     attend_back(
         {
-            2: [lambda: gather_far_b("F", gat_f, split_f)],
-            3: [lambda: gather_far_a("F", gat_f, split_f)],
+            1: [
+                lambda: transpose_into(wv, w3t, 2 * feats),
+                lambda: gather_near_by("F", gat_f, split_f),
+            ],
+            3: [
+                lambda: gather_cross_a("F", gat_f, split_f),
+            ],
+            4: [
+                lambda: gather_near_a("F", gat_f, split_f),
+            ],
+            7: [
+                lambda: gather_far_b("F", gat_f, split_f),
+                lambda: gather_far_a("F", gat_f, split_f),
+            ],
         }
     )
-
     multiply_out_b(far_x)
     reduce_far()
+    multiply_out_b(left_x)
     multiply_out_b(right_x)
+    reduce_left()
+    reduce_cross("f", far_x)
     reduce_right()
-    multiply_out_b(left_x)
-    reduce_left()
-    multiply_out_b(my_x)
-    reduce_mine()
+    reduce_cross("r", right_x)
     gather_end("F")
     project(gat_f)
-    reduce_near_a()
+    reduce_near_a(1)
     attend(far_x)
     swap_attn(far_x, "f")
+    reduce_cross("l", left_x)
+    attend(left_x)
+    swap_attn(left_x, "l")
     reduce_far_b()
     attend(right_x)
+    reduce_near_a(0)
+    multiply_out_b(my_x)
     swap_attn(right_x, "r")
-    attend(left_x)
-    swap_attn(left_x, "l")
-    reduce_cross_a()
+    reduce_cross("m", my_x)
     arrived("atf")
     multiply_out_f(far_x)
     row_far()
+    reduce_side_b()
+    arrived("atl")
+    multiply_out_f(left_x)
     reduce_near_b()
     arrived("atr")
     multiply_out_f(right_x)
-    row_right()
-    arrived("atl")
-    multiply_out_f(left_x)
-    row_left()
+    row_near(0)
+    row_right(0)
     attend(my_x)
+    row_left(0)
+    row_right(2)
     swap_attn(my_x, "m")
-    row_near()
-    finish_grad(last_a(), 0, "PBa")
-    finish_grad(last_b(), half, "PBb")
+    reduce_cross_a()
     arrived("atm")
     multiply_out_f(my_x)
-    arrived("RFf1Rd")
-    arrived("RFf1Li")
-    finish_act(0, "PFa")
-    arrived("RFf1Ri")
-    arrived("RFf1Ld")
-    finish_act(half, "PFb")
-    for name in ("PBa", "PBb", "PFa", "PFb"):
+    row_near(2)
+    row_left(2)
+    finish_grad(True)
+    row_near(1)
+    finish_act(0)
+    row_right(1)
+    row_left(1)
+    finish_grad(False)
+    finish_act(2)
+    finish_act(1)
+    for name in ("PBFalse", "PBTrue", "PF0", "PF1", "PF2"):
         arrived(name)
     for name in copies:
         describe(name).wait_send()
@@ -687,7 +739,7 @@
     cosine, sine = (jnp.asarray(table) for table in rope_constants(length))
     anywhere = pl.BlockSpec(memory_space=pl.ANY)
     vmem = pltpu.VMEM
-    n_copies = 104
+    n_copies = 112
     act, dgrad = pl.pallas_call(
         kernel,
         out_shape=[jax.ShapeDtypeStruct((rows, width), BF16)] * 2,

time: 148 us -> 132 us (0.89)
  Pallas kernels: 145 us -> 127 us
    pallas_call x1, Pallas kernels: 145 us -> 127 us  [shards(): pl.pallas_call(kernel, out_shape=[jax.ShapeDtypeStruct((rows, width), BF1...]
where the time goes in v4:
time: 132 us; the launch traced here: 131 us
  Pallas kernels  127 us (96%)
  other arithmetic  2.76 us (2%)
    pallas_call x1, Pallas kernels, shards(): pl.pallas_call(kernel, out_shape=[jax.ShapeDtypeStruct((rows, width), BF1...  127 us
    broadcast_in_dim x1, other arithmetic, shards(): return (act.astype(F32)[None], dgrad.astype(F32)[None])  2.76 us

profile of v4, /device:TPU:0, one launch (start us, length us, event | category | flops | bytes accessed | tf_op | source)
XLA Modules:
  0.0 130.7 jit_solution(11467014328914780448)
XLA Ops:
  0.6 127.3 %relay_attention.1 = (bf16[128,2048]{1,0:T(8,128)(2,1)}, bf16[128,2048]{1,0:T(8,128)(2,1)}) custom-call(f32[128,2048]{1,0:T(8,128)} %bitcast.13, f32[128,2048]{1,0:T(8,128)} %bitcast.14, f32[128,2048]{1,0:T(8,128)} %bitcast.15, f32[1,2048]{1,0:T(1,128)} %gain_ref.1, bf16[2048,256]{1,0:T(8,128)(2,1)} %bitcast.16, bf16[2048,256]{1,0:T(8,128)(2,1)} %bitcast.17, ...), custom_call_target="tpu_custom_call" | custom-call | tf_op jit(solution)/shard_map/relay_attention/pallas_call | solution.py:743
  127.9 2.8 %bitcast_convert_fusion = (f32[1,128,2048]{2,1,0:T(8,128)}, f32[1,128,2048]{2,1,0:T(8,128)}) fusion(bf16[128,2048]{1,0:T(8,128)(2,1)} %get-tuple-element.5, bf16[128,2048]{1,0:T(8,128)(2,1)} %get-tuple-element.4), kind=kLoop, calls=%fused_computation | loop fusion | flops 524288 | bytes 3145728 | tf_op jit(solution)/shard_map/broadcast_in_dim | solution.py:783

commit v5 on v4

--- a/solution.py
+++ b/solution.py
@@ -430,12 +430,11 @@
             out_f[here, :] = (x_fwd[here, :] + total).astype(BF16)
             return carry
 
-        lax.fori_loop(0, count // step_rows, body, 0)
-        send(
-            f"PF{number}",
-            lambda: (out_f.at[pl.ds(start, count)], act_ref.at[pl.ds(start, count)]),
-            "N",
-        )
+        piece = count // 2
+        for part in range(2):
+            lax.fori_loop(part * piece // step_rows, (part + 1) * piece // step_rows, body, 0)
+            here = pl.ds(start + part * piece, piece)
+            send(f"PF{number}{part}", lambda here=here: (out_f.at[here], act_ref.at[here]), "N")
 
     def finish_grad(last):
         if last:
@@ -726,7 +725,7 @@
     finish_grad(False)
     finish_act(2)
     finish_act(1)
-    for name in ("PBFalse", "PBTrue", "PF0", "PF1", "PF2"):
+    for name in ("PBFalse", "PBTrue", "PF00", "PF01", "PF10", "PF11", "PF20", "PF21"):
         arrived(name)
     for name in copies:
         describe(name).wait_send()
@@ -737,14 +736,14 @@
     feats = w_query.shape[2]
     length = rows * lax.axis_size("seq")
     cosine, sine = (jnp.asarray(table) for table in rope_constants(length))
-    anywhere = pl.BlockSpec(memory_space=pl.ANY)
+    hbm = pl.BlockSpec(memory_space=pltpu.HBM)
     vmem = pltpu.VMEM
     n_copies = 112
     act, dgrad = pl.pallas_call(
         kernel,
         out_shape=[jax.ShapeDtypeStruct((rows, width), BF16)] * 2,
-        in_specs=[anywhere] * 3 + [pl.BlockSpec(memory_space=pltpu.VMEM)] + [anywhere] * 6,
-        out_specs=[anywhere] * 2,
+        in_specs=[hbm] * 3 + [pl.BlockSpec(memory_space=pltpu.VMEM)] + [hbm] * 6,
+        out_specs=[pl.BlockSpec(memory_space=pltpu.VMEM)] * 2,
         scratch_shapes=[vmem((rows, width), F32)] * 3
         + [vmem((width, feats), BF16)] * 5
         + [vmem((length, HD), F32)] * 2
@@ -765,7 +764,7 @@
             pltpu.SemaphoreType.DMA((n_copies,)),
         ],
         compiler_params=pltpu.CompilerParams(
-            collective_id=0, has_side_effects=True, vmem_limit_bytes=67_043_328
+            collective_id=0, has_side_effects=True, vmem_limit_bytes=55_312_384
         ),
         name="relay_attention",
     )(

time: 132 us -> 131 us (level)
  no operation moved by 1% of the time
where the time goes in v5:
time: 131 us; the launch traced here: 129 us
  Pallas kernels  126 us (96%)
  other arithmetic  1.56 us (1%)
    pallas_call x1, Pallas kernels, shards(): pl.pallas_call(kernel, out_shape=[jax.ShapeDtypeStruct((rows, width), BF1...  126 us

profile of v5, /device:TPU:0, one launch (start us, length us, event | category | flops | bytes accessed | tf_op | source)
XLA Modules:
  0.0 129.3 jit_solution(12080750719335874816)
XLA Ops:
  0.6 0.0 copy-start
  0.6 0.7 copy-done
  1.3 126.4 %relay_attention.1 = (bf16[128,2048]{1,0:T(8,128)(2,1)S(1)}, bf16[128,2048]{1,0:T(8,128)(2,1)S(1)}) custom-call(f32[128,2048]{1,0:T(8,128)} %bitcast.13, f32[128,2048]{1,0:T(8,128)} %bitcast.14, f32[128,2048]{1,0:T(8,128)} %bitcast.15, f32[1,2048]{1,0:T(1,128)S(1)} %copy-done, bf16[2048,256]{1,0:T(8,128)(2,1)} %bitcast.16, bf16[2048,256]{1,0:T(8,128)(2,1)} %bitcast.17, ...), custom_call_target="tpu_custom_call" | custom-call | tf_op jit(solution)/shard_map/relay_attention/pallas_call | solution.py:742
  127.7 1.6 %bitcast_convert_fusion = (f32[1,128,2048]{2,1,0:T(8,128)}, f32[1,128,2048]{2,1,0:T(8,128)}) fusion(bf16[128,2048]{1,0:T(8,128)(2,1)S(1)} %get-tuple-element.5, bf16[128,2048]{1,0:T(8,128)(2,1)S(1)} %get-tuple-element.4), kind=kLoop, calls=%fused_computation | loop fusion | flops 524288 | bytes 3145728 | tf_op jit(solution)/shard_map/broadcast_in_dim | solution.py:782
Async XLA Ops:
  0.6 0.7 copy-start

commit v6 on v5

--- a/solution.py
+++ b/solution.py
@@ -117,12 +117,12 @@
         loads[index] = pltpu.make_async_copy(src, dst, load_sem.at[index])
         loads[index].start()
 
+    barrier = pltpu.get_barrier_semaphore()
+    for device in (devices[where] for where in "NPYLR"):
+        pl.semaphore_signal(barrier, inc=1, device_id=device, device_id_type=MESH)
+
     load(0, x_bwd_hbm, x_bwd)
     load(1, grad_hbm, grad)
-
-    barrier = pltpu.get_barrier_semaphore()
-    for device in devices.values():
-        pl.semaphore_signal(barrier, inc=1, device_id=device, device_id_type=MESH)
 
     copies = {}
 
@@ -725,10 +725,10 @@
     finish_grad(False)
     finish_act(2)
     finish_act(1)
+    for name in copies:
+        describe(name).wait_send()
     for name in ("PBFalse", "PBTrue", "PF00", "PF01", "PF10", "PF11", "PF20", "PF21"):
         arrived(name)
-    for name in copies:
-        describe(name).wait_send()
 
 
 def shards(x_fwd, x_bwd, grad_in, gain, w_query, w_key, w_value, w_out):

time: 131 us -> 130 us (level)
  no operation moved by 1% of the time
where the time goes in v6:
time: 130 us; the launch traced here: 129 us
  Pallas kernels  126 us (97%)
  other arithmetic  1.56 us (1%)
    pallas_call x1, Pallas kernels, shards(): pl.pallas_call(kernel, out_shape=[jax.ShapeDtypeStruct((rows, width), BF1...  126 us

profile of v6, /device:TPU:0, one launch (start us, length us, event | category | flops | bytes accessed | tf_op | source)
XLA Modules:
  0.0 129.1 jit_solution(7450952166630586023)
XLA Ops:
  0.6 0.0 copy-start
  0.6 0.7 copy-done
  1.3 126.2 %relay_attention.1 = (bf16[128,2048]{1,0:T(8,128)(2,1)S(1)}, bf16[128,2048]{1,0:T(8,128)(2,1)S(1)}) custom-call(f32[128,2048]{1,0:T(8,128)} %bitcast.13, f32[128,2048]{1,0:T(8,128)} %bitcast.14, f32[128,2048]{1,0:T(8,128)} %bitcast.15, f32[1,2048]{1,0:T(1,128)S(1)} %copy-done, bf16[2048,256]{1,0:T(8,128)(2,1)} %bitcast.16, bf16[2048,256]{1,0:T(8,128)(2,1)} %bitcast.17, ...), custom_call_target="tpu_custom_call" | custom-call | tf_op jit(solution)/shard_map/relay_attention/pallas_call | solution.py:742
  127.6 1.6 %bitcast_convert_fusion = (f32[1,128,2048]{2,1,0:T(8,128)}, f32[1,128,2048]{2,1,0:T(8,128)}) fusion(bf16[128,2048]{1,0:T(8,128)(2,1)S(1)} %get-tuple-element.5, bf16[128,2048]{1,0:T(8,128)(2,1)S(1)} %get-tuple-element.4), kind=kLoop, calls=%fused_computation | loop fusion | flops 524288 | bytes 3145728 | tf_op jit(solution)/shard_map/broadcast_in_dim | solution.py:782
Async XLA Ops:
  0.6 0.7 copy-start
